TPU v7x, 256 devices: a whole 4x4x8 slice. The times are simulated.
256 devices in a mesh: pipe: 4 (over x), expert: 64 (over y, z, core).
Axes of the slice: x: 4, y: 4, z: 8, core: 2. Of those that a mesh axis runs over, the one named last changes fastest.
Arguments:
- hidden_in: bfloat16 [4, 8192, 4096], P('pipe', 'expert'), may hold values from -90 to 90
- out_grad: bfloat16 [4, 8192, 4096], P('pipe', 'expert'), may hold values from -6 to 6
- expert_ids: int32 [4, 8192, 8], P('pipe', 'expert'), may hold values from 0 to 127, as said below
- route_weight: bfloat16 [4, 8192, 8], P('pipe', 'expert'), may hold values from 0.25 to 1
- norm_gain: float32 [4, 4096], P('pipe'), may hold values from 0.25 to 1.75
- w_gate_up: bfloat16 [4, 64, 2, 192, 4096], P('pipe', 'expert'), may hold values from -0.09375 to 0.09375
- w_down: bfloat16 [4, 64, 192, 4096], P('pipe', 'expert'), may hold values from -0.15625 to 0.15625
Outputs:
- handed_grad: bfloat16 [4, 8192, 4096], P('pipe', 'expert')
- grad_gate_up: bfloat16 [4, 64, 2, 192, 4096], P('pipe', 'expert')
- grad_down: bfloat16 [4, 64, 192, 4096], P('pipe', 'expert')
- grad_combine: float32 [4, 8192, 8], P('pipe', 'expert')
Inputs may be any that keep to these rules, and one draw needn't show every extreme that they name: `expert_ids`: each token names 8 different experts. In each layer, at most 8 tokens of one aligned block of 128 tokens name any one of the experts 0 to 7, and one of these experts is named by exactly 8 tokens of every block.
All inputs are finite; a program needn't handle non-finite values.
Results may differ from a plain program's by a relative error of at most 0.008.
Values may be sent and summed in bfloat16 or wider, within the bound.
A program may use at most 128 MiB of HBM per device.

v0:
```python
import jax
import jax.numpy as jnp
from jax import lax
from jax.sharding import PartitionSpec as P

SPLIT = 8
SPECIALIST_CAP = 8


def shifted(block, axis, distance):
    devices = range(lax.axis_size(axis))
    route = [((i - distance) % len(devices), i) for i in devices]
    return lax.ppermute(block, axis, route)


def rows_product(left_rows, right_rows):
    return lax.dot_general(
        left_rows, right_rows, (((1,), (1,)), ((), ())), preferred_element_type=jnp.float32
    )


def column_product(left_rows, right_rows):
    return lax.dot_general(
        left_rows, right_rows, (((0,), (0,)), ((), ())), preferred_element_type=jnp.float32
    )


def on_device(hidden_in, out_grad, expert_ids, route_weight, norm_gain, w_gate_up, w_down):
    tokens_in = hidden_in[0]
    grad_out = out_grad[0]
    chosen = expert_ids[0]
    weights_in = route_weight[0]
    gain_row = norm_gain[0]
    slab_gate_up = w_gate_up[0, 0]
    slab_down = w_down[0, 0]
    devices = lax.axis_size("expert")
    specialist_span = devices // SPLIT
    model_width = tokens_in.shape[1]
    hidden_slab = slab_down.shape[0]
    capacity = SPECIALIST_CAP
    tokens_f = tokens_in.astype(jnp.float32)
    rms_value = jnp.sqrt(jnp.mean(tokens_f * tokens_f, axis=-1, keepdims=True) + 1e-06)
    normed = tokens_f / rms_value
    normed_in = (normed * gain_row).astype(jnp.bfloat16)
    expert_range = jnp.arange(specialist_span, dtype=jnp.int32)
    picked = chosen[:, :, None] == expert_range[None, None, :]
    member = jnp.any(picked, axis=1).astype(jnp.int32)
    weight_te = jnp.sum(jnp.where(picked, weights_in.astype(jnp.float32)[:, :, None], 0.0), axis=1)
    position = jnp.cumsum(member, axis=0) - member
    slot_range = jnp.arange(capacity, dtype=jnp.int32)
    placing = (position.T[:, None, :] == slot_range[None, :, None]) & (member.T[:, None, :] == 1)
    place_bf = placing.astype(jnp.bfloat16)
    place_f = placing.astype(jnp.float32)
    sent_in = jnp.einsum(
        "wst,td->wsd", place_bf, normed_in, preferred_element_type=jnp.float32
    ).astype(jnp.bfloat16)
    sent_grad = jnp.einsum(
        "wst,td->wsd", place_bf, grad_out, preferred_element_type=jnp.float32
    ).astype(jnp.bfloat16)
    sent_weight = jnp.sum(place_f * weight_te.T[:, None, :], axis=-1).astype(jnp.bfloat16)
    rows_in, rows_grad, rows_weight = (
        lax.all_to_all(
            jnp.repeat(sent_in, SPLIT, axis=0), "expert", split_axis=0, concat_axis=0, tiled=True
        ),
        lax.all_to_all(
            jnp.repeat(sent_grad, SPLIT, axis=0), "expert", split_axis=0, concat_axis=0, tiled=True
        ),
        lax.all_to_all(
            jnp.repeat(sent_weight, SPLIT, axis=0),
            "expert",
            split_axis=0,
            concat_axis=0,
            tiled=True,
        ),
    )
    total_rows = devices * capacity
    flat_in = rows_in.reshape(total_rows, model_width)
    flat_grad = rows_grad.reshape(total_rows, model_width)
    flat_weight = rows_weight.reshape(total_rows, 1).astype(jnp.float32)
    joined_slab = slab_gate_up.reshape(2 * hidden_slab, model_width)
    projected = rows_product(flat_in, joined_slab)
    gate_pre = projected[:, :hidden_slab]
    up_pre = projected[:, hidden_slab:]
    sigmoid_gate = jax.nn.sigmoid(gate_pre)
    active = gate_pre * sigmoid_gate
    hidden_act = active * up_pre
    scaled_hidden = (flat_weight * hidden_act).astype(jnp.bfloat16)
    back_proj = rows_product(flat_grad, slab_down)
    grad_hidden = flat_weight * back_proj
    grad_gate = (
        grad_hidden * up_pre * sigmoid_gate * (1.0 + gate_pre * (1.0 - sigmoid_gate))
    ).astype(jnp.bfloat16)
    grad_up = (grad_hidden * active).astype(jnp.bfloat16)
    grad_both = jnp.concatenate([grad_gate, grad_up], axis=1)
    weight_grad = column_product(grad_both, flat_in)
    down_grad = column_product(scaled_hidden, flat_grad)
    input_part = (
        jnp.dot(grad_both, joined_slab, preferred_element_type=jnp.float32)
        .astype(jnp.bfloat16)
        .reshape(devices, capacity, model_width)
    )
    combine_part = (
        jnp.sum(hidden_act * back_proj, axis=-1).astype(jnp.bfloat16).reshape(devices, capacity)
    )
    returned_in, returned_comb = (
        lax.all_to_all(input_part, "expert", split_axis=0, concat_axis=0, tiled=True),
        lax.all_to_all(combine_part, "expert", split_axis=0, concat_axis=0, tiled=True),
    )
    summed_in = jnp.sum(
        returned_in.reshape(specialist_span, SPLIT, capacity, model_width).astype(jnp.float32),
        axis=1,
    )
    summed_comb = jnp.sum(
        returned_comb.reshape(specialist_span, SPLIT, capacity).astype(jnp.float32), axis=1
    )
    grad_normed = jnp.einsum("wst,wsd->td", place_f, summed_in, precision=lax.Precision.HIGHEST)
    comb_te = jnp.sum(place_f * summed_comb[:, :, None], axis=1)
    grad_combine = jnp.sum(jnp.where(picked, comb_te.T[:, None, :], 0.0), axis=-1)
    scaled = grad_normed * gain_row
    inner_mean = jnp.mean(scaled * normed, axis=-1, keepdims=True)
    grad_tokens = (
        grad_out.astype(jnp.float32) + (scaled - normed * inner_mean) / rms_value
    ).astype(jnp.bfloat16)
    handed = shifted(grad_tokens, "pipe", -1)
    gate_up_out = weight_grad.reshape(2, hidden_slab, model_width).astype(jnp.bfloat16)
    return (
        handed[None],
        gate_up_out[None, None],
        down_grad.astype(jnp.bfloat16)[None, None],
        grad_combine[None],
    )


def solution(mesh):
    return jax.shard_map(
        on_device,
        mesh=mesh,
        in_specs=(
            P("pipe", "expert", None),
            P("pipe", "expert", None),
            P("pipe", "expert", None),
            P("pipe", "expert", None),
            P("pipe", None),
            P("pipe", "expert", None, None, None),
            P("pipe", "expert", None, None),
        ),
        out_specs=(
            P("pipe", "expert", None),
            P("pipe", "expert", None, None, None),
            P("pipe", "expert", None, None),
            P("pipe", "expert", None),
        ),
        check_vma=False,
    )
```

profile of v0, /device:TPU:25, one launch (start us, length us, event | category | flops | bytes accessed | tf_op | source)
XLA Modules:
  0.0 395.0 jit_solution(17742722530763986663)
XLA Ops:
  0.6 0.0 copy-start
  0.6 0.8 fusion.19
  1.5 0.1 copy.45
  1.6 0.2 reduce_window_sum.11
  1.9 0.0 copy-start.6
  1.9 0.1 copy.47
  2.0 0.0 copy-start.9
  2.0 1.5 fusion.10
  3.5 0.0 copy-start.12
  3.5 1.7 convolution_convert_fusion.3
  5.3 0.0 copy-done.9
  5.3 0.0 copy-done.12
  5.3 2.5 broadcast_in_dim.57
  7.8 12.6 %all-to-all-start.2 = ((bf16[64,8,4096]{2,1,0:T(8,128)(2,1)}), bf16[64,8,4096]{2,1,0:T(8,128)(2,1)}, u32[]{:S(2)}, u32[]{:S(2)}) async-start(bf16[64,8,4096]{2,1,0:T(8,128)(2,1)} %bitcast.80), calls=%async_computation.2 | async-start | bytes 8388608 | tf_op jit(solution)/shard_map/all_to_all | solution.py:62
  20.4 2.3 convolution_convert_fusion.4
  22.7 93.4 %all-to-all-done.2 = bf16[64,8,4096]{2,1,0:T(8,128)(2,1)} async-done(((bf16[64,8,4096]{2,1,0:T(8,128)(2,1)}), bf16[64,8,4096]{2,1,0:T(8,128)(2,1)}, u32[]{:S(2)}, u32[]{:S(2)}) %all-to-all-start.2) | async-done | bytes 4194336 | tf_op jit(solution)/shard_map/all_to_all | solution.py:62
  116.1 3.5 broadcast_in_dim.56
  119.7 0.0 copy-start.11
  119.7 6.2 %all-to-all-start.1 = ((bf16[64,8,4096]{2,1,0:T(8,128)(2,1)}), bf16[64,8,4096]{2,1,0:T(8,128)(2,1)}, u32[]{:S(2)}, u32[]{:S(2)}) async-start(bf16[64,8,4096]{2,1,0:T(8,128)(2,1)} %bitcast.81), calls=%async_computation.1 | async-start | bytes 8388608 | tf_op jit(solution)/shard_map/all_to_all | solution.py:65
  125.9 0.0 copy-done.11
  125.9 0.0 copy-done
  125.9 4.9 %fusion.5 = f32[512,384]{0,1:T(8,128)} fusion(bf16[384,4096]{1,0:T(8,128)(2,1)S(1)} %bitcast.78, bf16[64,8,4096]{2,1,0:T(8,128)(2,1)} %all-to-all-done.2), kind=kOutput, calls=%fused_computation.12 | convolution fusion | flops 1610612736 | bytes 8126464 | tf_op jit(solution)/shard_map/dot_general | solution.py:17
  130.8 0.0 copy-start.4
  130.8 90.8 %all-to-all-done.1 = bf16[64,8,4096]{2,1,0:T(8,128)(2,1)} async-done(((bf16[64,8,4096]{2,1,0:T(8,128)(2,1)}), bf16[64,8,4096]{2,1,0:T(8,128)(2,1)}, u32[]{:S(2)}, u32[]{:S(2)}) %all-to-all-start.1) | async-done | bytes 4194336 | tf_op jit(solution)/shard_map/all_to_all | solution.py:65
  221.6 4.4 %multiply_reduce_fusion.1 = (bf16[512]{0:T(512)(128)(2,1)S(1)}, f32[512,192]{0,1:T(8,128)S(1)}) fusion(f32[512,384]{0,1:T(8,128)} %fusion.5, bf16[1,1,192,4096]{3,2,1,0:T(8,128)(2,1)} %param.13, bf16[64,8,4096]{2,1,0:T(8,128)(2,1)} %all-to-all-done.1), kind=kOutput, calls=%fused_computation.29 | convolution fusion | flops 805993984 | bytes 6947840 | tf_op jit(solution)/shard_map/dot_general | solution.py:17
  226.0 0.7 convert_element_type.130
  226.7 6.1 %all-to-all-start.4 = ((bf16[64,1,8]{2,1,0:T(2,128)(2,1)}), bf16[64,1,8]{2,1,0:T(2,128)(2,1)}, u32[]{:S(2)}, u32[]{:S(2)}) async-start(bf16[64,1,8]{2,1,0:T(2,128)(2,1)} %convert_element_type.130), calls=%async_computation.4 | async-start | bytes 65536 | tf_op jit(solution)/shard_map/all_to_all | solution.py:107
  232.7 0.0 copy-done.4
  232.8 7.2 %all-to-all-done.4 = bf16[64,1,8]{2,1,0:T(2,128)(2,1)} async-done(((bf16[64,1,8]{2,1,0:T(2,128)(2,1)}), bf16[64,1,8]{2,1,0:T(2,128)(2,1)}, u32[]{:S(2)}, u32[]{:S(2)}) %all-to-all-start.4) | async-done | bytes 1056 | tf_op jit(solution)/shard_map/all_to_all | solution.py:107
  239.9 0.8 convert_element_type.129
  240.7 0.1 copy.53
  240.8 0.0 copy-done.6
  240.8 1.4 select_reduce_fusion.1
  242.2 0.1 broadcast_in_dim.55
  242.2 0.7 all_to_all.19
  242.9 1.4 copy.48
  244.3 14.1 %all_to_all.30 = bf16[64,1,8]{2,1,0:T(2,128)(2,1)S(1)} all-to-all(bf16[64,1,8]{2,1,0:T(2,128)(2,1)} %copy.48), channel_id=1, replica_groups=mesh['pipe'=4,'expert'=64] {'expert'}, dimensions={0} | all-to-all | bytes 2048 | tf_op jit(solution)/shard_map/all_to_all | solution.py:68
  258.4 0.7 convert_reduce_fusion.1
  259.1 0.8 reshape.96
  259.9 1.3 multiply_convert_fusion.3
  261.3 2.4 fusion
  263.7 102.1 %all_to_all.31 = bf16[64,8,4096]{2,1,0:T(8,128)(2,1)S(1)} all-to-all(bf16[64,8,4096]{2,1,0:T(8,128)(2,1)S(1)} %fusion), channel_id=1, replica_groups=mesh['pipe'=4,'expert'=64] {'expert'}, dimensions={0} | all-to-all | bytes 8388608 | tf_op jit(solution)/shard_map/all_to_all | solution.py:106
  365.7 0.0 copy-start.14
  365.7 0.7 convert_reduce_fusion
  366.4 0.5 copy-done.1
  366.9 0.0 copy-done.7
  366.9 0.0 copy-done.10
  366.9 0.0 copy-done.13
  366.9 0.0 copy-done.14
  367.0 0.0 copy-start.2
  367.0 1.9 multiply_reduce_fusion
  368.9 0.0 copy-start.8
  368.9 0.0 copy-start.3
  369.0 0.0 copy-done.2
  369.0 0.7 add_convert_fusion
  369.6 2.5 collective-permute-start
  372.2 0.0 copy-done.5
  372.2 0.0 copy-done.8
  372.2 0.6 select_reduce_fusion
  372.8 0.0 copy-done.3
  372.8 4.4 %fusion.3 = bf16[1,1,192,4096]{3,2,1,0:T(8,128)(2,1)} fusion(bf16[64,8,4096]{2,1,0:T(8,128)(2,1)} %all-to-all-done.1, f32[512]{0:T(512)S(1)} %reshape.96, f32[512,384]{0,1:T(8,128)S(1)} %copy-done.3), kind=kOutput, calls=%fused_computation.8 | convolution fusion | flops 806780928 | bytes 6555648 | tf_op jit(solution)/shard_map/dot_general | solution.py:23
  377.2 5.7 %fusion.1 = bf16[1,1,2,192,4096]{4,3,2,1,0:T(8,128)(2,1)} fusion(bf16[2,192,512]{2,1,0:T(8,128)(2,1)S(1)} %bitcast.83, bf16[64,8,4096]{2,1,0:T(8,128)(2,1)} %all-to-all-done.2), kind=kOutput, calls=%fused_computation.4 | convolution fusion | flops 1612185600 | bytes 7733248 | tf_op jit(solution)/shard_map/dot_general | solution.py:23
  382.9 11.1 %collective-permute-done = bf16[128,4096]{1,0:T(8,128)(2,1)S(1)} collective-permute-done((bf16[128,4096]{1,0:T(8,128)(2,1)S(1)}, bf16[128,4096]{1,0:T(8,128)(2,1)S(1)}, u32[]{:S(2)}, u32[]{:S(2)}) %collective-permute-start) | collective-permute-done | bytes 1048608 | tf_op jit(solution)/shard_map/ppermute | solution.py:13
  394.0 1.0 copy.63
  (15 shorter events, 0.2 us)
Async XLA Ops:
  0.6 125.2 %copy-start = (bf16[1,1,2,192,4096]{4,3,2,1,0:T(8,128)(2,1)S(1)}, bf16[1,1,2,192,4096]{4,3,2,1,0:T(8,128)(2,1)}, u32[]{:S(2)}) copy-start(bf16[1,1,2,192,4096]{4,3,2,1,0:T(8,128)(2,1)} %param.12) | copy-start | bytes 9437188
  1.9 238.9 %copy-start.6 = (s32[8,128]{1,0:T(8,128)}, s32[8,128]{1,0:T(8,128)S(1)}, u32[]{:S(2)}) copy-start(s32[8,128]{1,0:T(8,128)S(1)} %copy.46) | copy-start | bytes 12292
  2.0 3.3 copy-start.9
  3.5 1.8 copy-start.12
  7.8 108.3 %all-to-all-start.2 = ((bf16[64,8,4096]{2,1,0:T(8,128)(2,1)}), bf16[64,8,4096]{2,1,0:T(8,128)(2,1)}, u32[]{:S(2)}, u32[]{:S(2)}) async-start(bf16[64,8,4096]{2,1,0:T(8,128)(2,1)} %bitcast.80), calls=%async_computation.2 | async-start | bytes 8388608 | tf_op jit(solution)/shard_map/all_to_all | solution.py:62
  119.7 6.2 %copy-start.11 = (bf16[1,128,8]{1,2,0:T(8,128)(2,1)S(1)}, bf16[1,128,8]{1,2,0:T(8,128)(2,1)}, u32[]{:S(2)}) copy-start(bf16[1,128,8]{1,2,0:T(8,128)(2,1)} %param.10) | copy-start | bytes 6148
  119.7 101.9 %all-to-all-start.1 = ((bf16[64,8,4096]{2,1,0:T(8,128)(2,1)}), bf16[64,8,4096]{2,1,0:T(8,128)(2,1)}, u32[]{:S(2)}, u32[]{:S(2)}) async-start(bf16[64,8,4096]{2,1,0:T(8,128)(2,1)} %bitcast.81), calls=%async_computation.1 | async-start | bytes 8388608 | tf_op jit(solution)/shard_map/all_to_all | solution.py:65
  130.8 102.0 %copy-start.4 = (s32[1,128,8]{1,2,0:T(8,128)S(1)}, s32[1,128,8]{1,2,0:T(8,128)}, u32[]{:S(2)}) copy-start(s32[1,128,8]{1,2,0:T(8,128)} %param.9) | copy-start | bytes 12292
  226.7 13.2 %all-to-all-start.4 = ((bf16[64,1,8]{2,1,0:T(2,128)(2,1)}), bf16[64,1,8]{2,1,0:T(2,128)(2,1)}, u32[]{:S(2)}, u32[]{:S(2)}) async-start(bf16[64,1,8]{2,1,0:T(2,128)(2,1)} %convert_element_type.130), calls=%async_computation.4 | async-start | bytes 65536 | tf_op jit(solution)/shard_map/all_to_all | solution.py:107
  365.7 1.2 copy-start.1
  365.7 1.2 copy-start.7
  365.7 1.2 copy-start.10
  365.7 1.2 copy-start.13
  365.7 1.2 copy-start.14
  367.0 2.0 copy-start.2
  368.9 3.3 copy-start.5
  368.9 3.3 copy-start.8
  368.9 3.9 copy-start.3
  369.6 24.4 %collective-permute-start = (bf16[128,4096]{1,0:T(8,128)(2,1)S(1)}, bf16[128,4096]{1,0:T(8,128)(2,1)S(1)}, u32[]{:S(2)}, u32[]{:S(2)}) collective-permute-start(bf16[128,4096]{1,0:T(8,128)(2,1)S(1)} %add_convert_fusion), channel_id=1, source_target_pairs={{64,0},{128,64},{192,128},{0,192},{65,1},{129,65},{193,129},{1,193... | collective-permute-start | bytes 3145736 | tf_op jit(solution)/shard_map/ppermute | solution.py:13
where the time goes:
time: 398 us; the launch traced here: 395 us
  waiting for transfers between devices  202 us (51%)
  blocking collectives  116 us (29%)
  matrix products  27.7 us (7%)
  starting transfers between devices  27.3 us (7%)
  local copies, waits for them, and re-layouts  11.6 us (3%)
  other arithmetic  8.83 us (2%)
    all_to_all x1, blocking collectives, on_device(): lax.all_to_all(input_part, 'expert', split_axis=0, concat_axis=0, tiled=T...  102 us
    all_to_all x1, waiting for transfers between devices, on_device(): lax.all_to_all(jnp.repeat(sent_in, SPLIT, axis=0), 'expert', split_axis=0...  93.4 us
    all_to_all x1, waiting for transfers between devices, on_device(): lax.all_to_all(jnp.repeat(sent_grad, SPLIT, axis=0), 'expert', split_axis...  90.8 us
    all_to_all x1, blocking collectives, on_device(): lax.all_to_all(jnp.repeat(sent_weight, SPLIT, axis=0), 'expert', split_ax...  14.1 us
    all_to_all x1, starting transfers between devices, on_device(): lax.all_to_all(jnp.repeat(sent_in, SPLIT, axis=0), 'expert', split_axis=0...  12.6 us
    ppermute x1, waiting for transfers between devices, shifted(): return lax.ppermute(block, axis, route)  11.1 us
    dot_general x2, matrix products, column_product(): lax.dot_general(left_rows, right_rows, (((0,), (0,)), ((), ())), preferre...  10.1 us
    dot_general x2, matrix products, rows_product(): lax.dot_general(left_rows, right_rows, (((1,), (1,)), ((), ())), preferre...  9.25 us
  transfers between devices with their start and end apart: 4, of which 4 were waited for; matrix products, arithmetic and copies ran while one was open for 5% of the time, Pallas kernels for 0%

commit v1 on v0

v1 whole, which is shorter than its diff:
```python
import jax
import jax.numpy as jnp
from jax import lax
from jax.experimental import pallas as pl
from jax.experimental.pallas import tpu as pltpu
from jax.sharding import PartitionSpec as P

SPLIT = 8
CAP = 8
NY = 4
NZ = 8
LINE = 4
MESH = pl.DeviceIdType.MESH
F32 = jnp.float32
BF16 = jnp.bfloat16


def nt(left, right):
    return lax.dot_general(left, right, (((1,), (1,)), ((), ())), preferred_element_type=F32)


def nn(left, right):
    return lax.dot_general(left, right, (((1,), (0,)), ((), ())), preferred_element_type=F32)


def tn(left, right):
    return lax.dot_general(left, right, (((0,), (0,)), ((), ())), preferred_element_type=F32)


def expert_kernel(
    mine_ref,
    wgu_hbm,
    wd_hbm,
    back_ref,
    ggu_hbm,
    gd_hbm,
    rows,
    wgu,
    wd,
    part,
    swap,
    summed,
    landed,
    da,
    db,
    hd,
    ggu,
    gd,
    row_sem,
    pair_sem,
    right_sem,
    left_sem,
    share_sem,
    entry_sem,
    swap_send,
    swap_recv,
    back_send,
    back_recv,
    w_sem,
    out_sem,
):
    me = lax.axis_index("expert")
    core = lax.rem(me, 2)
    z = lax.rem(me // 2, NZ)
    y = me // (2 * NZ)
    half = z // LINE
    pos = lax.rem(z, LINE)
    width = mine_ref.shape[2]
    hidden = wd.shape[0]
    halfw = width // 2
    outw = halfw + 128
    partner = me + 1 - 2 * core

    def at(yy, zz, cc):
        return (yy * NZ + zz) * 2 + cc

    barrier = pltpu.get_barrier_semaphore()

    @pl.loop(1, NY * NZ)
    def _(step):
        other = lax.rem(me // 2 + step, NY * NZ) * 2 + core
        pl.semaphore_signal(barrier, inc=1, device_id={"expert": other}, device_id_type=MESH)

    pl.semaphore_signal(barrier, inc=1, device_id={"expert": partner}, device_id_type=MESH)

    w_copies = [
        pltpu.make_async_copy(wgu_hbm, wgu, w_sem.at[0]),
        pltpu.make_async_copy(wd_hbm, wd, w_sem.at[1]),
    ]
    for copy in w_copies:
        copy.start()
    pl.semaphore_wait(barrier, NY * NZ)

    def remote(src, dst, send, recv, other):
        return pltpu.make_async_remote_copy(
            src_ref=src,
            dst_ref=dst,
            send_sem=send,
            recv_sem=recv,
            device_id={"expert": other},
            device_id_type=MESH,
        )

    def piece(kind, src_z, src_y):
        return rows.at[kind, src_z * NY + src_y]

    entry_z = jnp.where(pos >= 2, lax.rem(LINE * (half + 1), NZ), lax.rem(LINE * half + NZ - 1, NZ))
    slot = z * NY + y

    def entry(src_idx, sem_idx, other):
        return remote(
            mine_ref.at[src_idx], rows.at[core, slot], entry_sem.at[sem_idx], row_sem.at[slot], other
        )

    own_copy = pltpu.make_async_copy(mine_ref.at[y * 2 + half], rows.at[core, slot], row_sem.at[slot])
    own_copy.start()
    for step in range(NY):
        yy = lax.rem(y + step, NY)
        if step > 0:
            entry(yy * 2 + half, step, at(yy, z, core)).start()
        entry(yy * 2 + 1 - half, NY + step, at(yy, entry_z, core)).start()

    def forward(src_z, src_y, sems, sem_idx, other):
        return remote(
            piece(core, src_z, src_y),
            piece(core, src_z, src_y),
            sems.at[sem_idx],
            row_sem.at[src_z * NY + src_y],
            other,
        )

    def share(src_z, src_y):
        idx = src_z * NY + src_y
        return remote(
            piece(core, src_z, src_y),
            piece(core, src_z, src_y),
            share_sem.at[idx],
            pair_sem.at[idx],
            partner,
        )

    def arrived(src_z, src_y):
        idx = src_z * NY + src_y
        pltpu.make_async_copy(mine_ref.at[0], piece(core, src_z, src_y), row_sem.at[idx]).wait()

    right = at(y, lax.rem(z + 1, NZ), core)
    left = at(y, lax.rem(z + NZ - 1, NZ), core)

    @pl.loop(0, 6 * NY)
    def _(step):
        hop = step // NY
        src_y = lax.rem(y + lax.rem(step, NY), NY)
        from_left = lax.rem(z - hop + NZ, NZ)
        from_right = lax.rem(z + hop, NZ)

        @pl.when(hop <= pos + 2)
        def _():
            arrived(from_left, src_y)

            @pl.when(pos < LINE - 1)
            def _():
                forward(from_left, src_y, right_sem, step, right).start()

            @pl.when((hop == 0) & (pos > 0))
            def _():
                forward(from_left, src_y, left_sem, step, left).start()

            share(from_left, src_y).start()

        @pl.when((hop >= 1) & (hop <= 5 - pos))
        def _():
            arrived(from_right, src_y)

            @pl.when(pos > 0)
            def _():
                forward(from_right, src_y, left_sem, step, left).start()

            share(from_right, src_y).start()

    for copy in w_copies:
        copy.wait()

    pieces = 8
    chunk = pieces * 16
    my_half = pl.multiple_of(core * outw, 128)
    their_half = pl.multiple_of((1 - core) * outw, 128)

    def swap_copy(q):
        first = q * pieces
        return remote(
            part.at[pl.ds(first, pieces), :, pl.ds(their_half, outw)],
            swap.at[pl.ds(first, pieces)],
            swap_send.at[q],
            swap_recv.at[q],
            partner,
        )

    line_slot = (y * 2 + half) * LINE + pos

    def back_copy(idx):
        src_z = idx // NY
        src_y = lax.rem(idx, NY)
        return remote(
            summed.at[idx],
            landed.at[line_slot],
            back_send.at[idx],
            back_recv.at[line_slot],
            at(src_y, src_z, core),
        )

    def back_local(idx):
        return pltpu.make_async_copy(summed.at[idx], landed.at[line_slot], back_recv.at[line_slot])

    my_idx = z * NY + y

    def give_back(q):
        swap_copy(q).wait_recv()

        @pl.loop(0, pieces)
        def _(i):
            idx = q * pieces + i
            summed[idx] = (
                part[idx, :, pl.ds(my_half, outw)].astype(F32) + swap[idx].astype(F32)
            ).astype(BF16)

            @pl.when(idx == my_idx)
            def _():
                back_local(idx).start()

            @pl.when(idx != my_idx)
            def _():
                back_copy(idx).start()

    @pl.loop(0, 4)
    def _(order):
        q = lax.rem(z // 2 + 2 + order, 4)

        @pl.loop(0, pieces)
        def _(i):
            idx = q * pieces + i
            pltpu.make_async_copy(
                mine_ref.at[0], rows.at[1 - core, idx], pair_sem.at[idx]
            ).wait()

        u = rows[0, pl.ds(q * pieces, pieces)].reshape(chunk, width)
        dy = rows[1, pl.ds(q * pieces, pieces)].reshape(chunk, width)
        a = nt(u, wgu[0])
        b = nt(u, wgu[1])
        g = nt(dy, wd[...])
        sig = jax.nn.sigmoid(a)
        act = a * sig
        hdn = act * b
        dga = (g * b * sig * (1.0 + a * (1.0 - sig))).astype(BF16)
        dgb = (g * act).astype(BF16)
        where = pl.ds(pl.multiple_of(q * chunk, chunk), chunk)
        da[where] = dga
        db[where] = dgb
        hd[where] = hdn.astype(BF16)
        dc = jnp.sum(hdn * g, axis=1, keepdims=True)
        dc = jnp.broadcast_to(dc.astype(BF16), (chunk, 128)).reshape(pieces, 16, 128)
        for h in range(2):
            tile = 512
            for n in range(halfw // tile):
                col = h * halfw + n * tile
                du = nn(dga, wgu[0, :, col : col + tile]) + nn(dgb, wgu[1, :, col : col + tile])
                part[pl.ds(q * pieces, pieces), :, h * outw + n * tile : h * outw + (n + 1) * tile] = (
                    du.astype(BF16).reshape(pieces, 16, tile)
                )
            part[pl.ds(q * pieces, pieces), :, h * outw + halfw : (h + 1) * outw] = dc
        swap_copy(q).start()

        @pl.when(order > 0)
        def _():
            give_back(lax.rem(z // 2 + 1 + order, 4))

    give_back(lax.rem(z // 2 + 1, 4))

    tile = 512
    for n in range(width // tile):
        cols = slice(n * tile, (n + 1) * tile)
        u = rows[0, :, :, cols].reshape(-1, tile)
        dy = rows[1, :, :, cols].reshape(-1, tile)
        ggu[0, :, cols] = tn(da[...], u).astype(BF16)
        ggu[1, :, cols] = tn(db[...], u).astype(BF16)
        gd[:, cols] = tn(hd[...], dy).astype(BF16)
    out_copies = [
        pltpu.make_async_copy(ggu, ggu_hbm, out_sem.at[0]),
        pltpu.make_async_copy(gd, gd_hbm, out_sem.at[1]),
    ]
    for copy in out_copies:
        copy.start()

    for step in range(NY):
        if step > 0:
            entry(y * 2 + half, step, partner).wait_send()
        entry(y * 2 + 1 - half, NY + step, partner).wait_send()

    @pl.loop(0, 6 * NY)
    def _(step):
        hop = step // NY
        src_y = lax.rem(y + lax.rem(step, NY), NY)
        from_left = lax.rem(z - hop + NZ, NZ)
        from_right = lax.rem(z + hop, NZ)

        @pl.when((hop <= pos + 2) & (pos < LINE - 1))
        def _():
            forward(from_left, src_y, right_sem, step, right).wait_send()

        @pl.when((hop <= 5 - pos) & (pos > 0))
        def _():
            forward(from_right, src_y, left_sem, step, left).wait_send()

    @pl.loop(0, NY * NZ)
    def _(idx):
        share(idx // NY, lax.rem(idx, NY)).wait_send()

    @pl.loop(0, 4)
    def _(q):
        swap_copy(q).wait_send()

    @pl.loop(0, NY * 2)
    def _(e):
        total = jnp.zeros((16, outw), F32)
        for i in range(LINE):
            idx = e * LINE + i
            pltpu.make_async_copy(summed.at[0], landed.at[idx], back_recv.at[idx]).wait()
            total = total + landed[idx].astype(F32)
        back_ref[e] = total

    @pl.loop(0, NY * NZ)
    def _(idx):
        @pl.when(idx != my_idx)
        def _():
            back_copy(idx).wait_send()

    for copy in out_copies:
        copy.wait()


def experts(mine, wgu, wd):
    width = mine.shape[2]
    hidden = wd.shape[0]
    outw = width // 2 + 128
    slots = NY * NZ
    dma = pltpu.SemaphoreType.DMA
    return pl.pallas_call(
        expert_kernel,
        out_shape=(
            jax.ShapeDtypeStruct((NY * 2, 16, outw), F32),
            jax.ShapeDtypeStruct(wgu.shape, BF16),
            jax.ShapeDtypeStruct(wd.shape, BF16),
        ),
        in_specs=[
            pl.BlockSpec(memory_space=pltpu.VMEM),
            pl.BlockSpec(memory_space=pl.ANY),
            pl.BlockSpec(memory_space=pl.ANY),
        ],
        out_specs=(
            pl.BlockSpec(memory_space=pltpu.VMEM),
            pl.BlockSpec(memory_space=pl.ANY),
            pl.BlockSpec(memory_space=pl.ANY),
        ),
        scratch_shapes=[
            pltpu.VMEM((2, slots, 16, width), BF16),
            pltpu.VMEM(wgu.shape, BF16),
            pltpu.VMEM(wd.shape, BF16),
            pltpu.VMEM((slots, 16, 2 * outw), BF16),
            pltpu.VMEM((slots, 16, outw), BF16),
            pltpu.VMEM((slots, 16, outw), BF16),
            pltpu.VMEM((slots, 16, outw), BF16),
            pltpu.VMEM((slots * 16, hidden), BF16),
            pltpu.VMEM((slots * 16, hidden), BF16),
            pltpu.VMEM((slots * 16, hidden), BF16),
            pltpu.VMEM(wgu.shape, BF16),
            pltpu.VMEM(wd.shape, BF16),
            dma((slots,)),
            dma((slots,)),
            dma((6 * NY,)),
            dma((6 * NY,)),
            dma((slots,)),
            dma((2 * NY,)),
            dma((4,)),
            dma((4,)),
            dma((slots,)),
            dma((slots,)),
            dma((2,)),
            dma((2,)),
        ],
        compiler_params=pltpu.CompilerParams(
            collective_id=0, has_side_effects=True, vmem_limit_bytes=60 * 1024 * 1024
        ),
    )(mine, wgu, wd)


def on_device(hidden_in, out_grad, expert_ids, route_weight, norm_gain, w_gate_up, w_down):
    tokens_in = hidden_in[0]
    grad_out = out_grad[0]
    chosen = expert_ids[0]
    weights_in = route_weight[0]
    gain_row = norm_gain[0]
    devices = lax.axis_size("expert")
    span = devices // SPLIT
    width = tokens_in.shape[1]
    core = lax.rem(lax.axis_index("expert"), 2)
    pairs = [(i, i ^ 1) for i in range(devices)]

    tokens_f = tokens_in.astype(F32)
    rms_value = jnp.sqrt(jnp.mean(tokens_f * tokens_f, axis=-1, keepdims=True) + 1e-06)
    normed = tokens_f / rms_value
    normed_in = (normed * gain_row).astype(BF16)
    expert_range = jnp.arange(span, dtype=jnp.int32)
    picked = chosen[:, :, None] == expert_range[None, None, :]
    member = jnp.any(picked, axis=1).astype(jnp.int32)
    weight_te = jnp.sum(jnp.where(picked, weights_in.astype(F32)[:, :, None], 0.0), axis=1)
    position = jnp.cumsum(member, axis=0) - member
    slot_range = jnp.arange(CAP, dtype=jnp.int32)
    placing = (position.T[:, None, :] == slot_range[None, :, None]) & (member.T[:, None, :] == 1)
    place_f = placing.astype(F32)
    place_bf = placing.astype(BF16)
    place_w = (place_f * weight_te.T[:, None, :]).astype(BF16)
    sent_in = jnp.einsum("wst,td->wsd", place_bf, normed_in, preferred_element_type=F32).astype(BF16)
    sent_grad = jnp.einsum("wst,td->wsd", place_w, grad_out, preferred_element_type=F32).astype(BF16)
    keep = jnp.where(core == 0, sent_in, sent_grad)
    give = jnp.where(core == 0, sent_grad, sent_in)
    got = lax.ppermute(give, "expert", pairs)
    first = jnp.where(core == 0, keep, got)
    second = jnp.where(core == 0, got, keep)
    mine = jnp.concatenate([first, second], axis=1)

    back, grad_gate_up, grad_down = experts(mine, w_gate_up[0, 0], w_down[0, 0])

    rows_first, rows_second = back[:, :CAP], back[:, CAP:]
    keep = jnp.where(core == 0, rows_first, rows_second)
    give = jnp.where(core == 0, rows_second, rows_first)
    got = lax.ppermute(give.astype(BF16), "expert", pairs).astype(F32)
    halfw = width // 2
    low = jnp.where(core == 0, keep, got)
    high = jnp.where(core == 0, got, keep)
    summed_in = jnp.concatenate([low[:, :, :halfw], high[:, :, :halfw]], axis=-1)
    summed_comb = 0.5 * (low[:, :, halfw] + high[:, :, halfw])

    grad_normed = jnp.einsum("wst,wsd->td", place_f, summed_in, precision=lax.Precision.HIGHEST)
    comb_te = jnp.sum(place_f * summed_comb[:, :, None], axis=1)
    comb_te = comb_te / jnp.where(member.T == 1, weight_te.T, 1.0)
    grad_combine = jnp.sum(jnp.where(picked, comb_te.T[:, None, :], 0.0), axis=-1)
    scaled = grad_normed * gain_row
    inner_mean = jnp.mean(scaled * normed, axis=-1, keepdims=True)
    grad_tokens = (
        grad_out.astype(F32) + (scaled - normed * inner_mean) / rms_value
    ).astype(BF16)
    stages = lax.axis_size("pipe")
    handed = lax.ppermute(grad_tokens, "pipe", [((i + 1) % stages, i) for i in range(stages)])
    return (
        handed[None],
        grad_gate_up[None, None],
        grad_down[None, None],
        grad_combine[None],
    )


def solution(mesh):
    return jax.shard_map(
        on_device,
        mesh=mesh,
        in_specs=(
            P("pipe", "expert", None),
            P("pipe", "expert", None),
            P("pipe", "expert", None),
            P("pipe", "expert", None),
            P("pipe", None),
            P("pipe", "expert", None, None, None),
            P("pipe", "expert", None, None),
        ),
        out_specs=(
            P("pipe", "expert", None),
            P("pipe", "expert", None, None, None),
            P("pipe", "expert", None, None),
            P("pipe", "expert", None),
        ),
        check_vma=False,
    )
```

time: 398 us -> 197 us (0.49)
  the two profiles are of different devices: /device:TPU:25 before, /device:TPU:6 now
where the time goes in v1:
time: 197 us
  Pallas kernels  145 us (74%)
  waiting for transfers between devices  28 us (14%)
  other arithmetic  10 us (5%)
  local copies, waits for them, and re-layouts  7.91 us (4%)
  matrix products  4.08 us (2%)
    pallas_call x1, Pallas kernels, experts(): pl.pallas_call(expert_kernel, out_shape=(jax.ShapeDtypeStruct((NY * 2, 16...  145 us
    ppermute x1, waiting for transfers between devices, on_device(): lax.ppermute(grad_tokens, 'pipe', [((i + 1) % stages, i) for i in range(s...  24.7 us
    unnamed x13, local copies, waits for them, and re-layouts  7.2 us
  transfers between devices with their start and end apart: 3, of which 3 were waited for; matrix products, arithmetic and copies ran while one was open for 1% of the time, Pallas kernels for 0%

profile of v1, /device:TPU:6, one launch (start us, length us, event | category | flops | bytes accessed | tf_op | source)
XLA Modules:
  0.0 197.1 jit_solution(10217482558749873240)
XLA Ops:
  0.6 0.7 fusion.9
  1.3 0.1 copy.39
  1.5 0.2 reduce_window_sum.11
  1.7 0.1 copy.41
  1.8 1.5 fusion.1
  3.3 0.7 bitcast_convert_fusion
  4.0 0.7 select_reduce_fusion.2
  4.8 0.0 copy-start.1
  4.8 1.8 convolution_convert_fusion.1
  6.6 0.0 copy-done.1
  6.6 0.3 broadcast_select_fusion.2
  6.9 0.1 collective-permute-start
  7.0 1.9 collective-permute-done
  8.9 0.1 broadcast_select_fusion.1
  9.0 1.0 pad_maximum_fusion.mine_ref
  10.1 145.2 %shard_map.102 = (f32[8,16,2176]{2,1,0:T(8,128)}, bf16[2,192,4096]{2,1,0:T(8,128)(2,1)}, bf16[192,4096]{1,0:T(8,128)(2,1)}) custom-call(bf16[8,16,4096]{2,1,0:T(8,128)(2,1)} %pad_maximum_fusion.mine_ref, bf16[2,192,4096]{2,1,0:T(8,128)(2,1)} %bitcast.45, bf16[192,4096]{1,0:T(8,128)(2,1)} %bitcast.47), custom_call_target="tpu_custom_call" | custom-call | tf_op jit(solution)/shard_map/pallas_call | solution.py:346
  155.2 1.3 select_convert_fusion
  156.5 0.3 collective-permute-start.1
  156.8 1.4 collective-permute-done.1
  158.2 1.3 convert_select_fusion.1
  159.5 0.0 copy-start
  159.5 0.0 copy-start.4
  159.6 0.1 pad_maximum_fusion.1
  159.7 1.0 copy-done
  160.7 0.0 copy-done.4
  160.7 2.0 multiply_reduce_fusion
  162.7 0.0 copy-start.3
  162.7 1.6 add_convert_fusion
  164.3 0.8 collective-permute-start.2
  165.2 0.1 copy.47
  165.3 0.1 copy.49
  165.4 0.1 select_reduce_fusion.1
  165.5 0.1 copy.46
  165.7 0.0 copy-done.3
  165.7 0.6 select_reduce_fusion
  166.3 24.7 %collective-permute-done.2 = bf16[128,4096]{1,0:T(8,128)(2,1)S(1)} collective-permute-done((bf16[128,4096]{1,0:T(8,128)(2,1)}, bf16[128,4096]{1,0:T(8,128)(2,1)S(1)}, u32[]{:S(2)}, u32[]{:S(2)}) %collective-permute-start.2) | collective-permute-done | bytes 1048608 | tf_op jit(solution)/shard_map/ppermute | solution.py:452
  191.0 1.0 copy.63
  192.0 0.0 copy-start.2
  192.0 4.0 %copy.64 = bf16[1,1,2,192,4096]{4,3,2,1,0:T(8,128)(2,1)} copy(bf16[1,1,2,192,4096]{4,3,2,1,0:T(8,128)(2,1)} %bitcast.44) | data formatting | bytes 6291456
  196.0 0.0 copy-done.2
  196.0 1.1 copy.65
  (12 shorter events, 0.3 us)
Async XLA Ops:
  4.8 1.9 copy-start.1
  6.9 2.0 %collective-permute-start = (bf16[8,8,4096]{2,1,0:T(8,128)(2,1)S(1)}, bf16[8,8,4096]{2,1,0:T(8,128)(2,1)S(1)}, u32[]{:S(2)}, u32[]{:S(2)}) collective-permute-start(bf16[8,8,4096]{2,1,0:T(8,128)(2,1)S(1)} %get-tuple-element.16), channel_id=1, source_target_pairs={{0,1},{1,0},{2,3},{3,2},{4,5},{5,4},{6,7},{7,6},{8,9},{9,8},{10,11... | collective-permute-start | bytes 1572872 | tf_op jit(solution)/shard_map/ppermute | solution.py:425
  156.5 1.6 collective-permute-start.1
  159.5 1.2 copy-start
  159.5 1.2 copy-start.4
  162.7 3.0 %copy-start.3 = (s32[1,128,8]{1,2,0:T(8,128)S(1)}, s32[1,128,8]{1,2,0:T(8,128)}, u32[]{:S(2)}) copy-start(s32[1,128,8]{1,2,0:T(8,128)} %param.9) | copy-start | bytes 12292
  164.3 26.7 %collective-permute-start.2 = (bf16[128,4096]{1,0:T(8,128)(2,1)}, bf16[128,4096]{1,0:T(8,128)(2,1)S(1)}, u32[]{:S(2)}, u32[]{:S(2)}) collective-permute-start(bf16[128,4096]{1,0:T(8,128)(2,1)} %add_convert_fusion), channel_id=1, source_target_pairs={{64,0},{128,64},{192,128},{0,192},{65,1},{129,65},{193,129},{1,193... | collective-permute-start | bytes 3145736 | tf_op jit(solution)/shard_map/ppermute | solution.py:452
  192.0 4.0 %copy-start.2 = (bf16[192,4096]{1,0:T(8,128)(2,1)S(1)}, bf16[192,4096]{1,0:T(8,128)(2,1)}, u32[]{:S(2)}) copy-start(bf16[192,4096]{1,0:T(8,128)(2,1)} %get-tuple-element.9) | copy-start | bytes 4718596

commit v2 on v1

v2 whole, which is shorter than its diff:
```python
import jax
import jax.numpy as jnp
from jax import lax
from jax.experimental import pallas as pl
from jax.experimental.pallas import tpu as pltpu
from jax.sharding import PartitionSpec as P

SPLIT = 8
CAP = 8
NY = 4
NZ = 8
LINE = 4
MESH = pl.DeviceIdType.MESH
F32 = jnp.float32
BF16 = jnp.bfloat16


def nt(left, right):
    return lax.dot_general(left, right, (((1,), (1,)), ((), ())), preferred_element_type=F32)


def nn(left, right):
    return lax.dot_general(left, right, (((1,), (0,)), ((), ())), preferred_element_type=F32)


def tn(left, right):
    return lax.dot_general(left, right, (((0,), (0,)), ((), ())), preferred_element_type=F32)


def expert_kernel(
    mine_ref,
    wgu_hbm,
    wd_hbm,
    hidden_ref,
    grad_ref,
    gain_ref,
    place_ref,
    back_ref,
    ggu_hbm,
    gd_hbm,
    hidden_next,
    grad_next,
    gain_next,
    place_next,
    rows,
    wgu,
    wd,
    part,
    swap,
    chain,
    summed,
    final,
    acc,
    da,
    db,
    hd,
    ggu,
    gd,
    row_sem,
    pair_sem,
    right_sem,
    left_sem,
    share_sem,
    entry_sem,
    swap_send,
    swap_recv,
    chain_send,
    chain_recv,
    final_send,
    back_recv,
    w_sem,
    out_sem,
    early_send,
    early_recv,
):
    me = lax.axis_index("expert")
    stage = lax.axis_index("pipe")
    stages = lax.axis_size("pipe")
    before = lax.rem(stage + stages - 1, stages)
    after = lax.rem(stage + 1, stages)
    core = lax.rem(me, 2)
    z = lax.rem(me // 2, NZ)
    y = me // (2 * NZ)
    half = z // LINE
    pos = lax.rem(z, LINE)
    expert = y * 2 + half
    width = mine_ref.shape[2]
    halfw = width // 2
    outw = halfw + 128
    slots = NY * NZ
    last = LINE - 1
    at_end = (pos == 0) | (pos == last)

    def at(yy, zz, cc):
        return (yy * NZ + zz) * 2 + cc

    partner = at(y, z, 1 - core)
    right = at(y, lax.rem(z + 1, NZ), core)
    left = at(y, lax.rem(z + NZ - 1, NZ), core)
    entry_z = jnp.where(pos >= 2, lax.rem(LINE * (half + 1), NZ), lax.rem(LINE * half + NZ - 1, NZ))

    barrier = pltpu.get_barrier_semaphore()

    def greet(pipe, other):
        pl.semaphore_signal(
            barrier, inc=1, device_id={"pipe": pipe, "expert": other}, device_id_type=MESH
        )

    greet(stage, partner)
    for step in range(1, NY):
        greet(stage, at(lax.rem(y + step, NY), z, core))

    @pl.when(pos > 0)
    def _():
        greet(stage, left)

    @pl.when(pos < last)
    def _():
        greet(stage, right)

    @pl.when(at_end)
    def _():
        way = jnp.where(pos == 0, NZ - 1, 1)
        for hop in (1, 2):
            for yy in range(NY):
                greet(stage, at(yy, lax.rem(z + hop * way, NZ), core))

    for cc in range(2):
        for yy in range(NY):
            greet(after, at(yy, z, cc))
            greet(after, at(yy, entry_z, cc))

    w_copies = [
        pltpu.make_async_copy(wgu_hbm, wgu, w_sem.at[0]),
        pltpu.make_async_copy(wd_hbm, wd, w_sem.at[1]),
    ]
    for copy in w_copies:
        copy.start()
    common = 1 + (NY - 1) + NY + 2 * NY
    pl.semaphore_wait(barrier, jnp.where(at_end, common + 1 + 4 * NY, common + 2))

    def remote(src, dst, send, recv, other, pipe=None):
        return pltpu.make_async_remote_copy(
            src_ref=src,
            dst_ref=dst,
            send_sem=send,
            recv_sem=recv,
            device_id={"pipe": stage if pipe is None else pipe, "expert": other},
            device_id_type=MESH,
        )

    slot = z * NY + y

    def entry(src_idx, sem_idx, other):
        return remote(
            mine_ref.at[src_idx], rows.at[core, slot], entry_sem.at[sem_idx], row_sem.at[slot], other
        )

    own_copy = pltpu.make_async_copy(mine_ref.at[expert], rows.at[core, slot], row_sem.at[slot])
    own_copy.start()
    for step in range(NY):
        yy = lax.rem(y + step, NY)
        if step > 0:
            entry(yy * 2 + half, step, at(yy, z, core)).start()
        entry(yy * 2 + 1 - half, NY + step, at(yy, entry_z, core)).start()

    early = [
        remote(src, dst, early_send.at[i], early_recv.at[i], me, before)
        for i, (src, dst) in enumerate(
            (
                (hidden_ref, hidden_next),
                (grad_ref, grad_next),
                (gain_ref, gain_next),
                (place_ref, place_next),
            )
        )
    ]
    for copy in early:
        copy.start()

    def piece(idx):
        return rows.at[core, idx]

    def forward(idx, sems, sem_idx, other):
        return remote(piece(idx), piece(idx), sems.at[sem_idx], row_sem.at[idx], other)

    def share(idx):
        return remote(piece(idx), piece(idx), share_sem.at[idx], pair_sem.at[idx], partner)

    def arrived(idx):
        pltpu.make_async_copy(mine_ref.at[0], piece(idx), row_sem.at[idx]).wait()

    def z_of(offset):
        return lax.rem(z + offset + NZ, NZ)

    my_half = pl.multiple_of(core * outw, 128)
    their_half = pl.multiple_of((1 - core) * outw, 128)
    block = NY * 16

    def swap_copy(src_z):
        span = pl.ds(src_z * NY, NY)
        return remote(
            part.at[span, :, pl.ds(their_half, outw)],
            swap.at[span],
            swap_send.at[src_z],
            swap_recv.at[src_z],
            partner,
        )

    def compute(src_z):
        @pl.loop(0, NY)
        def _(j):
            idx = src_z * NY + j
            pltpu.make_async_copy(
                mine_ref.at[0], rows.at[1 - core, idx], pair_sem.at[idx]
            ).wait()

        span = pl.ds(src_z * NY, NY)
        u = rows[0, span].reshape(block, width)
        dy = rows[1, span].reshape(block, width)
        a = nt(u, wgu[0])
        b = nt(u, wgu[1])
        g = nt(dy, wd[...])
        sig = jax.nn.sigmoid(a)
        act = a * sig
        hdn = act * b
        dga = (g * b * sig * (1.0 + a * (1.0 - sig))).astype(BF16)
        dgb = (g * act).astype(BF16)
        where = pl.ds(pl.multiple_of(src_z * block, block), block)
        da[where] = dga
        db[where] = dgb
        hd[where] = hdn.astype(BF16)
        dc = jnp.sum(hdn * g, axis=1, keepdims=True)
        dc = jnp.broadcast_to(dc.astype(BF16), (block, 128)).reshape(NY, 16, 128)
        part[span, :, :128] = dc
        part[span, :, width + 128 :] = dc
        tile = 512
        for n in range(width // tile):
            du = nn(dga, wgu[0, :, n * tile : (n + 1) * tile]) + nn(
                dgb, wgu[1, :, n * tile : (n + 1) * tile]
            )
            part[span, :, 128 + n * tile : 128 + (n + 1) * tile] = du.astype(BF16).reshape(
                NY, 16, tile
            )
        swap_copy(src_z).start()

    def chain_in(idx):
        pltpu.make_async_copy(summed.at[0], chain.at[idx], chain_recv.at[idx]).wait()
        acc[...] += chain[idx].astype(F32)

    def chain_out(idx, dst, other):
        return remote(summed.at[idx], chain.at[dst], chain_send.at[idx], chain_recv.at[dst], other)

    def final_out(number, cc, src_y, src_z):
        return remote(
            final.at[number, pl.ds(cc * CAP, CAP)],
            back_ref.at[expert, :, pl.ds(my_half, outw)],
            final_send.at[2 * number + cc],
            back_recv.at[2 * expert + core],
            at(src_y, src_z, cc),
            before,
        )

    def finish(number, src_y, src_z):
        final[number] = acc[...]
        for cc in range(2):
            final_out(number, cc, src_y, src_z).start()

    def combine(src_z, hop, kind):
        swap_copy(src_z).wait_recv()

        @pl.loop(0, NY)
        def _(j):
            idx = src_z * NY + j
            acc[...] = part[idx, :, pl.ds(my_half, outw)].astype(F32) + swap[idx].astype(F32)
            if kind == 0:

                @pl.when(pos < last)
                def _():
                    chain_in(idx)

                @pl.when(pos > 0)
                def _():
                    chain_in(slots + j)

                finish(j, j, src_z)
            elif kind < 0:

                @pl.when(pos < last)
                def _():
                    chain_in(idx)

                @pl.when(pos > 0)
                def _():
                    summed[idx] = acc[...].astype(BF16)
                    chain_out(idx, idx, left).start()

                @pl.when(pos == 0)
                def _():
                    finish(hop * NY + j, j, src_z)
            else:

                @pl.when(pos > 0)
                def _():
                    chain_in(idx)

                @pl.when(pos < last)
                def _():
                    summed[idx] = acc[...].astype(BF16)
                    chain_out(idx, jnp.where(hop == 1, slots + j, idx), right).start()

                @pl.when(pos == last)
                def _():
                    finish(hop * NY + j, j, src_z)

    wait_own = 2 + 2 * jnp.where(pos >= 2, pos, last - pos)

    @pl.loop(0, 11)
    def _(it):
        @pl.when(it <= 5)
        def _():
            @pl.loop(0, NY)
            def _(j):
                src_y = lax.rem(y + j, NY)
                number = it * NY + j
                from_left = z_of(-it) * NY + src_y
                from_right = z_of(it) * NY + src_y

                @pl.when(it <= pos + 2)
                def _():
                    arrived(from_left)

                    @pl.when(pos < last)
                    def _():
                        forward(from_left, right_sem, number, right).start()

                    @pl.when((it == 0) & (pos > 0))
                    def _():
                        forward(from_left, left_sem, number, left).start()

                    share(from_left).start()

                @pl.when((it >= 1) & (it <= 5 - pos))
                def _():
                    arrived(from_right)

                    @pl.when(pos > 0)
                    def _():
                        forward(from_right, left_sem, number, left).start()

                    share(from_right).start()

        @pl.when(it == 1)
        def _():
            for copy in w_copies:
                copy.wait()

        hop = it - 1

        @pl.loop(0, 2)
        def _(way):
            @pl.when(
                (hop <= 5)
                & (hop >= way)
                & (hop <= jnp.where(way == 0, pos + 2, 5 - pos))
            )
            def _():
                compute(z_of(jnp.where(way == 0, -hop, hop)))

        hop_l = it - 2 - 2 * (last - pos)

        @pl.when((hop_l >= 1) & (hop_l <= pos + 2))
        def _():
            combine(z_of(-hop_l), hop_l, -1)

        hop_r = it - 2 - 2 * pos

        @pl.when((hop_r >= 1) & (hop_r <= 5 - pos))
        def _():
            combine(z_of(hop_r), hop_r, 1)

        @pl.when(it == wait_own)
        def _():
            combine(z, 0, 0)

        @pl.loop(0, 2)
        def _(s):
            n = 2 * (it - 6) - 1 + s
            tile = 512

            @pl.when((n >= 0) & (n < width // tile))
            def _():
                cols = pl.ds(pl.multiple_of(n * tile, tile), tile)
                u = rows[0, :, :, cols].reshape(-1, tile)
                dy = rows[1, :, :, cols].reshape(-1, tile)
                ggu[0, :, cols] = tn(da[...], u).astype(BF16)
                ggu[1, :, cols] = tn(db[...], u).astype(BF16)
                gd[:, cols] = tn(hd[...], dy).astype(BF16)

    out_copies = [
        pltpu.make_async_copy(ggu, ggu_hbm, out_sem.at[0]),
        pltpu.make_async_copy(gd, gd_hbm, out_sem.at[1]),
    ]
    for copy in out_copies:
        copy.start()

    for step in range(NY):
        if step > 0:
            entry(expert, step, partner).wait_send()
        entry(expert, NY + step, partner).wait_send()
    for copy in early:
        copy.wait()

    @pl.loop(0, 6)
    def _(hop):
        from_left = z_of(-hop)
        from_right = z_of(hop)

        @pl.loop(0, NY)
        def _(j):
            src_y = lax.rem(y + j, NY)

            @pl.when((hop <= pos + 2) & (pos < last))
            def _():
                forward(from_left * NY + src_y, right_sem, hop * NY + j, right).wait_send()

            @pl.when((hop <= 5 - pos) & (pos > 0))
            def _():
                forward(from_right * NY + src_y, left_sem, hop * NY + j, left).wait_send()

            @pl.when((hop >= 1) & (hop <= pos + 2) & (pos > 0))
            def _():
                idx = from_left * NY + j
                chain_out(idx, idx, left).wait_send()

            @pl.when((hop >= 1) & (hop <= 5 - pos) & (pos < last))
            def _():
                idx = from_right * NY + j
                chain_out(idx, idx, right).wait_send()

            @pl.when((hop == 0) | ((hop <= 2) & at_end))
            def _():
                for cc in range(2):
                    final_out(hop * NY + j, cc, j, z).wait_send()

    @pl.loop(0, slots)
    def _(idx):
        share(idx).wait_send()

    @pl.loop(0, NZ)
    def _(src_z):
        swap_copy(src_z).wait_send()

    for e in range(NY * 2):
        for cc in range(2):
            pltpu.make_async_copy(
                final.at[0, pl.ds(0, CAP)],
                back_ref.at[e, :, pl.ds(cc * outw, outw)],
                back_recv.at[2 * e + cc],
            ).wait()
    for copy in out_copies:
        copy.wait()


def experts(mine, wgu, wd, hidden, grad, gain, place):
    width = mine.shape[2]
    units = wd.shape[0]
    outw = width // 2 + 128
    slots = NY * NZ
    dma = pltpu.SemaphoreType.DMA
    hbm = pl.BlockSpec(memory_space=pl.ANY)
    vmem = pl.BlockSpec(memory_space=pltpu.VMEM)
    like = lambda array: jax.ShapeDtypeStruct(array.shape, array.dtype)
    return pl.pallas_call(
        expert_kernel,
        out_shape=(
            jax.ShapeDtypeStruct((NY * 2, CAP, 2 * outw), F32),
            like(wgu),
            like(wd),
            like(hidden),
            like(grad),
            like(gain),
            like(place),
        ),
        in_specs=[vmem] + [hbm] * 6,
        out_specs=[vmem] + [hbm] * 6,
        scratch_shapes=[
            pltpu.VMEM((2, slots, 16, width), BF16),
            pltpu.VMEM(wgu.shape, BF16),
            pltpu.VMEM(wd.shape, BF16),
            pltpu.VMEM((slots, 16, 2 * outw), BF16),
            pltpu.VMEM((slots, 16, outw), BF16),
            pltpu.VMEM((slots + NY, 16, outw), BF16),
            pltpu.VMEM((slots, 16, outw), BF16),
            pltpu.VMEM((3 * NY, 16, outw), F32),
            pltpu.VMEM((16, outw), F32),
            pltpu.VMEM((slots * 16, units), BF16),
            pltpu.VMEM((slots * 16, units), BF16),
            pltpu.VMEM((slots * 16, units), BF16),
            pltpu.VMEM(wgu.shape, BF16),
            pltpu.VMEM(wd.shape, BF16),
            dma((slots,)),
            dma((slots,)),
            dma((6 * NY,)),
            dma((6 * NY,)),
            dma((slots,)),
            dma((2 * NY,)),
            dma((NZ,)),
            dma((NZ,)),
            dma((slots,)),
            dma((slots + NY,)),
            dma((6 * NY,)),
            dma((4 * NY,)),
            dma((2,)),
            dma((2,)),
            dma((4,)),
            dma((4,)),
        ],
        compiler_params=pltpu.CompilerParams(
            collective_id=0, has_side_effects=True, vmem_limit_bytes=60 * 1024 * 1024
        ),
    )(mine, wgu, wd, hidden, grad, gain, place)


def on_device(hidden_in, out_grad, expert_ids, route_weight, norm_gain, w_gate_up, w_down):
    tokens_in = hidden_in[0]
    grad_out = out_grad[0]
    chosen = expert_ids[0]
    weights_in = route_weight[0]
    gain_row = norm_gain[0]
    devices = lax.axis_size("expert")
    span = devices // SPLIT
    width = tokens_in.shape[1]
    core = lax.rem(lax.axis_index("expert"), 2)
    pairs = [(i, i ^ 1) for i in range(devices)]

    tokens_f = tokens_in.astype(F32)
    rms_value = jnp.sqrt(jnp.mean(tokens_f * tokens_f, axis=-1, keepdims=True) + 1e-06)
    normed = tokens_f / rms_value
    normed_in = (normed * gain_row).astype(BF16)
    expert_range = jnp.arange(span, dtype=jnp.int32)
    picked = chosen[:, :, None] == expert_range[None, None, :]
    member = jnp.any(picked, axis=1).astype(jnp.int32)
    weight_te = jnp.sum(jnp.where(picked, weights_in.astype(F32)[:, :, None], 0.0), axis=1)
    position = jnp.cumsum(member, axis=0) - member
    slot_range = jnp.arange(CAP, dtype=jnp.int32)
    placing = (position.T[:, None, :] == slot_range[None, :, None]) & (member.T[:, None, :] == 1)
    place_f = placing.astype(F32)
    place_bf = placing.astype(BF16)
    place_w = (place_f * weight_te.T[:, None, :]).astype(BF16)
    sent_in = jnp.einsum("wst,td->wsd", place_bf, normed_in, preferred_element_type=F32).astype(BF16)
    sent_grad = jnp.einsum("wst,td->wsd", place_w, grad_out, preferred_element_type=F32).astype(BF16)
    keep = jnp.where(core == 0, sent_in, sent_grad)
    give = jnp.where(core == 0, sent_grad, sent_in)
    got = lax.ppermute(give, "expert", pairs)
    first = jnp.where(core == 0, keep, got)
    second = jnp.where(core == 0, got, keep)
    mine = jnp.concatenate([first, second], axis=1)

    back, grad_gate_up, grad_down, hidden_next, grad_next, gain_next, place_next = experts(
        mine,
        w_gate_up[0, 0],
        w_down[0, 0],
        tokens_in,
        grad_out,
        gain_row.reshape(-1, 128),
        place_bf.reshape(span * CAP, -1),
    )

    stages = lax.axis_size("pipe")
    comb_rows = lax.ppermute(
        back[:, :, 0], "pipe", [(i, (i + 1) % stages) for i in range(stages)]
    )
    summed_in = back[:, :, 128 : width + 128].reshape(span * CAP, width)
    grad_normed = lax.dot_general(
        place_next.astype(F32),
        summed_in,
        (((0,), (0,)), ((), ())),
        precision=lax.Precision.HIGHEST,
        preferred_element_type=F32,
    )
    next_f = hidden_next.astype(F32)
    next_rms = jnp.sqrt(jnp.mean(next_f * next_f, axis=-1, keepdims=True) + 1e-06)
    next_normed = next_f / next_rms
    scaled = grad_normed * gain_next.reshape(width)
    inner_mean = jnp.mean(scaled * next_normed, axis=-1, keepdims=True)
    handed = (
        grad_next.astype(F32) + (scaled - next_normed * inner_mean) / next_rms
    ).astype(BF16)

    comb_te = jnp.sum(place_f * comb_rows[:, :, None], axis=1)
    comb_te = comb_te / jnp.where(member.T == 1, weight_te.T, 1.0)
    grad_combine = jnp.sum(jnp.where(picked, comb_te.T[:, None, :], 0.0), axis=-1)
    return (
        handed[None],
        grad_gate_up[None, None],
        grad_down[None, None],
        grad_combine[None],
    )


def solution(mesh):
    return jax.shard_map(
        on_device,
        mesh=mesh,
        in_specs=(
            P("pipe", "expert", None),
            P("pipe", "expert", None),
            P("pipe", "expert", None),
            P("pipe", "expert", None),
            P("pipe", None),
            P("pipe", "expert", None, None, None),
            P("pipe", "expert", None, None),
        ),
        out_specs=(
            P("pipe", "expert", None),
            P("pipe", "expert", None, None, None),
            P("pipe", "expert", None, None),
            P("pipe", "expert", None),
        ),
        check_vma=False,
    )
```

time: 197 us -> 158 us (0.80)
  the two profiles are of different devices: /device:TPU:6 before, /device:TPU:61 now
where the time goes in v2:
time: 158 us
  Pallas kernels  134 us (85%)
  other arithmetic  9.54 us (6%)
  matrix products  5.24 us (3%)
  local copies, waits for them, and re-layouts  5.13 us (3%)
  starting transfers between devices  2.88 us (2%)
    pallas_call x1, Pallas kernels, experts(): pl.pallas_call(expert_kernel, out_shape=(jax.ShapeDtypeStruct((NY * 2, CA...  134 us
    unnamed x14, local copies, waits for them, and re-layouts  3.71 us
  transfers between devices with their start and end apart: 2, of which 1 were waited for; matrix products, arithmetic and copies ran while one was open for 4% of the time, Pallas kernels for 0%

profile of v2, /device:TPU:61, one launch (start us, length us, event | category | flops | bytes accessed | tf_op | source)
XLA Modules:
  0.0 157.8 jit_solution(14740029211923366921)
XLA Ops:
  0.6 1.5 fusion
  2.2 0.7 fusion.13
  2.9 0.7 bitcast_convert_fusion
  3.6 0.7 select_reduce_fusion.2
  4.3 0.1 copy.27
  4.4 0.1 copy.29
  4.5 0.2 reduce_window_sum.11
  4.7 0.0 copy-start
  4.7 1.9 %convolution_convert_fusion.1 = bf16[8,8,4096]{2,1,0:T(8,128)(2,1)S(1)} fusion(f32[4096]{0:T(1024)} %bitcast.60, f32[128]{0:T(128)S(1)} %add_sqrt_fusion.1, s32[8,128]{1,0:T(8,128)S(1)} %copy.28, pred[8,128]{1,0:T(8,128)(4,1)S(1)} %copy.29, bf16[1,128,4096]{2,1,0:T(8,128)(2,1)} %param.7), kind=kOutput, calls=%fused_computation.2 | convolution fusion | flops 69484544 | bytes 1594880 | tf_op jit(solution)/shard_map/wst,td->wsd/dot_general | solution.py:551
  6.6 0.0 copy-done
  6.6 0.3 broadcast_select_fusion.2
  6.9 0.8 collective-permute-start
  7.6 0.1 copy.31
  7.8 0.1 eq.71
  7.8 0.7 fusion.17.place_ref
  8.5 0.7 collective-permute-done
  9.2 0.1 broadcast_select_fusion.1
  9.3 1.0 pad_maximum_fusion.mine_ref
  10.3 133.6 %shard_map.102 = (f32[8,8,4352]{2,1,0:T(8,128)}, bf16[2,192,4096]{2,1,0:T(8,128)(2,1)}, bf16[192,4096]{1,0:T(8,128)(2,1)}, bf16[128,4096]{1,0:T(8,128)(2,1)}, bf...) custom-call(bf16[8,16,4096]{2,1,0:T(8,128)(2,1)} %pad_maximum_fusion.mine_ref, ...), custom_call_target="tpu_custom_call" | custom-call | tf_op jit(solution)/shard_map/pallas_call | solution.py:474
  143.9 1.5 fusion.3
  145.5 0.8 slice_reduce_fusion
  146.3 2.1 %collective-permute-start.1 = (f32[8,8]{1,0:T(8,128)S(1)}, f32[8,8]{1,0:T(8,128)S(1)}, u32[]{:S(2)}, u32[]{:S(2)}) collective-permute-start(f32[8,8]{1,0:T(8,128)S(1)} %slice_reduce_fusion), channel_id=1, source_target_pairs={{0,64},{64,128},{128,192},{192,0},{1,65},{65,129},{129,193},{193,1... | collective-permute-start | bytes 776 | tf_op jit(solution)/shard_map/ppermute | solution.py:571
  148.4 0.0 copy-start.1
  148.4 0.0 copy-start.4
  148.4 3.1 %multiply_reduce_fusion = (f32[128]{0:T(128)S(1)}, f32[128,4096]{1,0:T(8,128)S(1)}) fusion(bf16[128,4096]{1,0:T(8,128)(2,1)} %get-tuple-element.15, f32[128]{0:T(128)S(1)} %add_sqrt_fusion, f32[4096]{0:T(1024)} %bitcast.63, bf16[64,128]{1,0:T(8,128)(2,1)} %get-tuple-element.12, f32[8,8,4352]{2,1,0:T(8,128)} %get-tuple-element.13), kind=kOutput, calls=%fused_computation.12 | convolution fusion | flops 405274496 | bytes 4228096 | tf_op jit(solution)/shard_map/dot_general | solution.py:575
  151.6 0.0 copy-done.1
  151.6 0.0 copy-done.4
  151.6 0.0 copy-start.5
  151.6 0.0 copy-start.2
  151.6 1.6 %fusion.11 = bf16[1,128,4096]{2,1,0:T(8,128)(2,1)} fusion(f32[128,4096]{1,0:T(8,128)S(1)} %get-tuple-element.25, f32[128]{0:T(128)S(1)} %broadcast_multiply_fusion, f32[128]{0:T(128)S(1)} %add_sqrt_fusion, bf16[128,4096]{1,0:T(8,128)(2,1)S(1)} %copy-done.1, bf16[128,4096]{1,0:T(8,128)(2,1)S(1)} %copy-done.4), kind=kLoop, calls=%fused_computation.20 | loop fusion | flops 4194304 | bytes 5243904 | tf_op jit(solution)/shard_map/broadcast_in_dim | solution.py:595
  153.2 0.0 collective-permute-done.1
  153.2 0.1 select_reduce_fusion.1
  153.3 0.1 copy.30
  153.5 0.0 copy-done.5
  153.5 0.6 select_reduce_fusion
  154.1 0.0 copy-done.2
  154.1 0.0 copy-start.3
  154.1 1.7 %copy.35 = bf16[1,1,2,192,4096]{4,3,2,1,0:T(8,128)(2,1)} copy(bf16[1,1,2,192,4096]{4,3,2,1,0:T(8,128)(2,1)S(1)} %bitcast.52) | data formatting | bytes 6291456
  155.8 0.9 copy-done.3
  156.7 1.1 copy.36
  (9 shorter events, 0.2 us)
Async XLA Ops:
  4.7 1.9 %copy-start = (bf16[1,128,4096]{2,1,0:T(8,128)(2,1)S(1)}, bf16[1,128,4096]{2,1,0:T(8,128)(2,1)}, u32[]{:S(2)}) copy-start(bf16[1,128,4096]{2,1,0:T(8,128)(2,1)} %param.8) | copy-start | bytes 3145732
  6.9 2.3 %collective-permute-start = (bf16[8,8,4096]{2,1,0:T(8,128)(2,1)S(1)}, bf16[8,8,4096]{2,1,0:T(8,128)(2,1)S(1)}, u32[]{:S(2)}, u32[]{:S(2)}) collective-permute-start(bf16[8,8,4096]{2,1,0:T(8,128)(2,1)S(1)} %get-tuple-element.22), channel_id=1, source_target_pairs={{0,1},{1,0},{2,3},{3,2},{4,5},{5,4},{6,7},{7,6},{8,9},{9,8},{10,11... | collective-permute-start | bytes 1572872 | tf_op jit(solution)/shard_map/ppermute | solution.py:555
  146.3 6.9 %collective-permute-start.1 = (f32[8,8]{1,0:T(8,128)S(1)}, f32[8,8]{1,0:T(8,128)S(1)}, u32[]{:S(2)}, u32[]{:S(2)}) collective-permute-start(f32[8,8]{1,0:T(8,128)S(1)} %slice_reduce_fusion), channel_id=1, source_target_pairs={{0,64},{64,128},{128,192},{192,0},{1,65},{65,129},{129,193},{193,1... | collective-permute-start | bytes 776 | tf_op jit(solution)/shard_map/ppermute | solution.py:571
  148.4 3.1 %copy-start.1 = (bf16[128,4096]{1,0:T(8,128)(2,1)S(1)}, bf16[128,4096]{1,0:T(8,128)(2,1)}, u32[]{:S(2)}) copy-start(bf16[128,4096]{1,0:T(8,128)(2,1)} %get-tuple-element.15) | copy-start | bytes 3145732
  148.4 3.1 %copy-start.4 = (bf16[128,4096]{1,0:T(8,128)(2,1)S(1)}, bf16[128,4096]{1,0:T(8,128)(2,1)}, u32[]{:S(2)}) copy-start(bf16[128,4096]{1,0:T(8,128)(2,1)} %get-tuple-element.11) | copy-start | bytes 3145732
  151.6 1.9 %copy-start.5 = (s32[1,128,8]{1,2,0:T(8,128)S(1)}, s32[1,128,8]{1,2,0:T(8,128)}, u32[]{:S(2)}) copy-start(s32[1,128,8]{1,2,0:T(8,128)} %param.9) | copy-start | bytes 12292
  151.6 2.5 %copy-start.2 = (bf16[2,192,4096]{2,1,0:T(8,128)(2,1)S(1)}, bf16[2,192,4096]{2,1,0:T(8,128)(2,1)}, u32[]{:S(2)}) copy-start(bf16[2,192,4096]{2,1,0:T(8,128)(2,1)} %get-tuple-element.16) | copy-start | bytes 9437188
  154.1 2.5 %copy-start.3 = (bf16[192,4096]{1,0:T(8,128)(2,1)S(1)}, bf16[192,4096]{1,0:T(8,128)(2,1)}, u32[]{:S(2)}) copy-start(bf16[192,4096]{1,0:T(8,128)(2,1)} %get-tuple-element.17) | copy-start | bytes 4718596

commit v3 on v2

--- a/solution.py
+++ b/solution.py
@@ -181,8 +181,8 @@
     def piece(idx):
         return rows.at[core, idx]
 
-    def forward(idx, sems, sem_idx, other):
-        return remote(piece(idx), piece(idx), sems.at[sem_idx], row_sem.at[idx], other)
+    def forward(idx, sems, other):
+        return remote(piece(idx), piece(idx), sems.at[idx], row_sem.at[idx], other)
 
     def share(idx):
         return remote(piece(idx), piece(idx), share_sem.at[idx], pair_sem.at[idx], partner)
@@ -262,7 +262,7 @@
         )
 
     def finish(number, src_y, src_z):
-        final[number] = acc[...]
+        final[number] = acc[...].astype(BF16)
         for cc in range(2):
             final_out(number, cc, src_y, src_z).start()
 
@@ -313,79 +313,111 @@
                 def _():
                     finish(hop * NY + j, j, src_z)
 
-    wait_own = 2 + 2 * jnp.where(pos >= 2, pos, last - pos)
-
-    @pl.loop(0, 11)
+    def list_at(place, slot):
+        near = jnp.where(slot == 1, place - 1, jnp.where(slot == 5, 1, place + 4 - slot))
+        return jnp.where(place < 2, place + 3 - slot, near)
+
+    def origin(slot):
+        return jnp.where(slot == 1, 1, jnp.where(slot == 5, 2, slot - 4))
+
+    flip = last - pos
+
+    def own_idx(j):
+        return z * NY + lax.rem(y + NY - j, NY)
+
+    @pl.loop(0, 16)
     def _(it):
-        @pl.when(it <= 5)
+        slot_now = it // 2
+        part_now = lax.rem(it, 2)
+
+        for jj in range(2):
+            j = 2 * part_now + jj
+            src_y = lax.rem(y + NY - j, NY)
+
+            @pl.when(slot_now == 0)
+            def _():
+                idx = own_idx(j)
+                arrived(idx)
+
+                @pl.when(pos == 1)
+                def _():
+                    forward(idx, right_sem, right).start()
+
+                @pl.when(pos == 2)
+                def _():
+                    forward(idx, left_sem, left).start()
+
+                share(idx).start()
+
+            @pl.when((slot_now >= 1) & (slot_now <= pos + 2))
+            def _():
+                idx = z_of(-list_at(pos, slot_now)) * NY + src_y
+                arrived(idx)
+
+                @pl.when(pos < last)
+                def _():
+                    forward(idx, right_sem, right).start()
+
+                share(idx).start()
+
+            @pl.when((slot_now >= 1) & (slot_now <= flip + 2))
+            def _():
+                idx = z_of(list_at(flip, slot_now)) * NY + src_y
+                arrived(idx)
+
+                @pl.when(pos > 0)
+                def _():
+                    forward(idx, left_sem, left).start()
+
+                share(idx).start()
+
+        @pl.when(((it == 5) & (pos == 0)) | ((it == 9) & (pos == 2)))
         def _():
-            @pl.loop(0, NY)
-            def _(j):
-                src_y = lax.rem(y + j, NY)
-                number = it * NY + j
-                from_left = z_of(-it) * NY + src_y
-                from_right = z_of(it) * NY + src_y
-
-                @pl.when(it <= pos + 2)
-                def _():
-                    arrived(from_left)
-
-                    @pl.when(pos < last)
-                    def _():
-                        forward(from_left, right_sem, number, right).start()
-
-                    @pl.when((it == 0) & (pos > 0))
-                    def _():
-                        forward(from_left, left_sem, number, left).start()
-
-                    share(from_left).start()
-
-                @pl.when((it >= 1) & (it <= 5 - pos))
-                def _():
-                    arrived(from_right)
-
-                    @pl.when(pos > 0)
-                    def _():
-                        forward(from_right, left_sem, number, left).start()
-
-                    share(from_right).start()
-
-        @pl.when(it == 1)
+            for j in range(NY):
+                forward(own_idx(j), right_sem, right).start()
+
+        @pl.when(((it == 5) & (flip == 0)) | ((it == 9) & (flip == 2)))
+        def _():
+            for j in range(NY):
+                forward(own_idx(j), left_sem, left).start()
+
+        @pl.when(it == 2)
         def _():
             for copy in w_copies:
                 copy.wait()
 
-        hop = it - 1
-
-        @pl.loop(0, 2)
-        def _(way):
-            @pl.when(
-                (hop <= 5)
-                & (hop >= way)
-                & (hop <= jnp.where(way == 0, pos + 2, 5 - pos))
-            )
-            def _():
-                compute(z_of(jnp.where(way == 0, -hop, hop)))
-
-        hop_l = it - 2 - 2 * (last - pos)
-
-        @pl.when((hop_l >= 1) & (hop_l <= pos + 2))
+        slot_done = slot_now - 1
+        limit = jnp.where(part_now == 0, pos + 2, flip + 2)
+
+        @pl.when((slot_done >= part_now) & (slot_done <= limit) & (slot_done <= 5))
         def _():
-            combine(z_of(-hop_l), hop_l, -1)
-
-        hop_r = it - 2 - 2 * pos
-
-        @pl.when((hop_r >= 1) & (hop_r <= 5 - pos))
+            place = jnp.where(part_now == 0, pos, flip)
+            away = jnp.where(slot_done == 0, 0, list_at(place, slot_done))
+            compute(z_of(jnp.where(part_now == 0, -away, away)))
+
+        since_l = it - 3 - flip
+        slot_l = since_l // 2
+        away_l = pos - origin(slot_l)
+
+        @pl.when((since_l >= 2) & (lax.rem(since_l + 2, 2) == 0) & (slot_l <= 5) & (away_l >= 1))
         def _():
-            combine(z_of(hop_r), hop_r, 1)
-
-        @pl.when(it == wait_own)
+            combine(z_of(-away_l), away_l, -1)
+
+        since_r = it - 4 - pos
+        slot_r = since_r // 2
+        away_r = flip - origin(slot_r)
+
+        @pl.when((since_r >= 2) & (lax.rem(since_r + 2, 2) == 0) & (slot_r <= 5) & (away_r >= 1))
+        def _():
+            combine(z_of(away_r), away_r, 1)
+
+        @pl.when(it == 14 + lax.rem(pos, 2))
         def _():
             combine(z, 0, 0)
 
-        @pl.loop(0, 2)
+        @pl.loop(0, 3)
         def _(s):
-            n = 2 * (it - 6) - 1 + s
+            n = 3 * (it - 13) - 1 + s
             tile = 512
 
             @pl.when((n >= 0) & (n < width // tile))
@@ -418,15 +450,13 @@
 
         @pl.loop(0, NY)
         def _(j):
-            src_y = lax.rem(y + j, NY)
-
             @pl.when((hop <= pos + 2) & (pos < last))
             def _():
-                forward(from_left * NY + src_y, right_sem, hop * NY + j, right).wait_send()
+                forward(from_left * NY + j, right_sem, right).wait_send()
 
             @pl.when((hop <= 5 - pos) & (pos > 0))
             def _():
-                forward(from_right * NY + src_y, left_sem, hop * NY + j, left).wait_send()
+                forward(from_right * NY + j, left_sem, left).wait_send()
 
             @pl.when((hop >= 1) & (hop <= pos + 2) & (pos > 0))
             def _():
@@ -474,7 +504,7 @@
     return pl.pallas_call(
         expert_kernel,
         out_shape=(
-            jax.ShapeDtypeStruct((NY * 2, CAP, 2 * outw), F32),
+            jax.ShapeDtypeStruct((NY * 2, CAP, 2 * outw), BF16),
             like(wgu),
             like(wd),
             like(hidden),
@@ -492,7 +522,7 @@
             pltpu.VMEM((slots, 16, outw), BF16),
             pltpu.VMEM((slots + NY, 16, outw), BF16),
             pltpu.VMEM((slots, 16, outw), BF16),
-            pltpu.VMEM((3 * NY, 16, outw), F32),
+            pltpu.VMEM((3 * NY, 16, outw), BF16),
             pltpu.VMEM((16, outw), F32),
             pltpu.VMEM((slots * 16, units), BF16),
             pltpu.VMEM((slots * 16, units), BF16),
@@ -501,8 +531,8 @@
             pltpu.VMEM(wd.shape, BF16),
             dma((slots,)),
             dma((slots,)),
-            dma((6 * NY,)),
-            dma((6 * NY,)),
+            dma((slots,)),
+            dma((slots,)),
             dma((slots,)),
             dma((2 * NY,)),
             dma((NZ,)),
@@ -569,15 +599,11 @@
 
     stages = lax.axis_size("pipe")
     comb_rows = lax.ppermute(
-        back[:, :, 0], "pipe", [(i, (i + 1) % stages) for i in range(stages)]
+        back[:, :, 0].astype(F32), "pipe", [(i, (i + 1) % stages) for i in range(stages)]
     )
     summed_in = back[:, :, 128 : width + 128].reshape(span * CAP, width)
     grad_normed = lax.dot_general(
-        place_next.astype(F32),
-        summed_in,
-        (((0,), (0,)), ((), ())),
-        precision=lax.Precision.HIGHEST,
-        preferred_element_type=F32,
+        place_next, summed_in, (((0,), (0,)), ((), ())), preferred_element_type=F32
     )
     next_f = hidden_next.astype(F32)
     next_rms = jnp.sqrt(jnp.mean(next_f * next_f, axis=-1, keepdims=True) + 1e-06)

time: 158 us -> 192 us (1.22)
  the two profiles are of different devices: /device:TPU:61 before, /device:TPU:25 now
where the time goes in v3:
time: 192 us; the launch traced here: 189 us
  Pallas kernels  166 us (86%)
  other arithmetic  10.3 us (5%)
  matrix products  4.31 us (2%)
  local copies, waits for them, and re-layouts  4.28 us (2%)
  starting transfers between devices  1.98 us (1%)
    pallas_call x1, Pallas kernels, experts(): pl.pallas_call(expert_kernel, out_shape=(jax.ShapeDtypeStruct((NY * 2, CA...  166 us
  transfers between devices with their start and end apart: 2, of which 2 were waited for; matrix products, arithmetic and copies ran while one was open for 2% of the time, Pallas kernels for 0%

profile of v3, /device:TPU:25, one launch (start us, length us, event | category | flops | bytes accessed | tf_op | source)
XLA Modules:
  0.0 189.0 jit_solution(3885451287697833172)
XLA Ops:
  0.6 1.5 fusion
  2.2 0.7 fusion.13
  2.9 0.7 bitcast_convert_fusion
  3.6 0.7 select_reduce_fusion.2
  4.3 0.1 copy.27
  4.4 0.1 copy.29
  4.5 0.2 reduce_window_sum.11
  4.7 0.0 copy-start
  4.7 1.9 convolution_convert_fusion.1
  6.6 0.0 copy-done
  6.6 0.3 broadcast_select_fusion.2
  6.9 0.8 collective-permute-start
  7.6 0.1 copy.31
  7.8 0.1 eq.71
  7.8 0.7 fusion.17.place_ref
  8.5 0.7 collective-permute-done
  9.2 0.1 broadcast_select_fusion.1
  9.3 1.0 pad_maximum_fusion.mine_ref
  10.3 165.7 %shard_map.102 = (bf16[8,8,4352]{2,1,0:T(8,128)(2,1)}, bf16[2,192,4096]{2,1,0:T(8,128)(2,1)}, bf16[192,4096]{1,0:T(8,128)(2,1)}, bf16[128,4096]{1,0:T(8,128)(2,1...) custom-call(bf16[8,16,4096]{2,1,0:T(8,128)(2,1)} %pad_maximum_fusion.mine_ref, ...), custom_call_target="tpu_custom_call" | custom-call | tf_op jit(solution)/shard_map/pallas_call | solution.py:504
  176.0 1.5 fusion.3
  177.6 0.8 convert_reduce_fusion
  178.4 1.2 collective-permute-start.1
  179.6 0.0 copy-start.1
  179.6 0.0 copy-start.4
  179.6 2.2 %multiply_reduce_fusion = (f32[128]{0:T(128)S(1)}, f32[128,4096]{1,0:T(8,128)S(1)}) fusion(bf16[128,4096]{1,0:T(8,128)(2,1)} %get-tuple-element.15, f32[128]{0:T(128)S(1)} %add_sqrt_fusion, f32[4096]{0:T(1024)} %bitcast.63, bf16[64,128]{1,0:T(8,128)(2,1)} %get-tuple-element.12, bf16[8,8,4352]{2,1,0:T(8,128)(2,1)} %get-tuple-element.13), kind=kOutput, calls=%fused_computation.12 | convolution fusion | flops 69730176 | bytes 3703808 | tf_op jit(solution)/shard_map/dot_general | solution.py:605
  181.8 0.0 copy-done.1
  181.8 0.0 copy-done.4
  181.8 0.0 copy-start.5
  181.8 0.0 copy-start.2
  181.8 1.6 fusion.9
  183.4 1.0 collective-permute-done.1
  184.5 0.1 select_reduce_fusion.1
  184.6 0.1 copy.30
  184.7 0.0 copy-done.5
  184.7 0.6 select_reduce_fusion
  185.4 0.0 copy-done.2
  185.4 0.0 copy-start.3
  185.4 1.7 copy.35
  187.0 0.9 copy-done.3
  187.9 1.1 copy.36
  (9 shorter events, 0.2 us)
Async XLA Ops:
  4.7 1.9 copy-start
  6.9 2.3 %collective-permute-start = (bf16[8,8,4096]{2,1,0:T(8,128)(2,1)S(1)}, bf16[8,8,4096]{2,1,0:T(8,128)(2,1)S(1)}, u32[]{:S(2)}, u32[]{:S(2)}) collective-permute-start(bf16[8,8,4096]{2,1,0:T(8,128)(2,1)S(1)} %get-tuple-element.22), channel_id=1, source_target_pairs={{0,1},{1,0},{2,3},{3,2},{4,5},{5,4},{6,7},{7,6},{8,9},{9,8},{10,11... | collective-permute-start | bytes 1572872 | tf_op jit(solution)/shard_map/ppermute | solution.py:585
  178.4 6.1 %collective-permute-start.1 = (f32[8,8]{1,0:T(8,128)S(1)}, f32[8,8]{1,0:T(8,128)S(1)}, u32[]{:S(2)}, u32[]{:S(2)}) collective-permute-start(f32[8,8]{1,0:T(8,128)S(1)} %convert_reduce_fusion), channel_id=1, source_target_pairs={{0,64},{64,128},{128,192},{192,0},{1,65},{65,129},{129,193},{193,1... | collective-permute-start | bytes 776 | tf_op jit(solution)/shard_map/ppermute | solution.py:601
  179.6 2.2 %copy-start.1 = (bf16[128,4096]{1,0:T(8,128)(2,1)S(1)}, bf16[128,4096]{1,0:T(8,128)(2,1)}, u32[]{:S(2)}) copy-start(bf16[128,4096]{1,0:T(8,128)(2,1)} %get-tuple-element.15) | copy-start | bytes 3145732
  179.6 2.2 %copy-start.4 = (bf16[128,4096]{1,0:T(8,128)(2,1)S(1)}, bf16[128,4096]{1,0:T(8,128)(2,1)}, u32[]{:S(2)}) copy-start(bf16[128,4096]{1,0:T(8,128)(2,1)} %get-tuple-element.11) | copy-start | bytes 3145732
  181.8 2.9 %copy-start.5 = (s32[1,128,8]{1,2,0:T(8,128)S(1)}, s32[1,128,8]{1,2,0:T(8,128)}, u32[]{:S(2)}) copy-start(s32[1,128,8]{1,2,0:T(8,128)} %param.9) | copy-start | bytes 12292
  181.8 3.6 %copy-start.2 = (bf16[2,192,4096]{2,1,0:T(8,128)(2,1)S(1)}, bf16[2,192,4096]{2,1,0:T(8,128)(2,1)}, u32[]{:S(2)}) copy-start(bf16[2,192,4096]{2,1,0:T(8,128)(2,1)} %get-tuple-element.16) | copy-start | bytes 9437188
  185.4 2.5 %copy-start.3 = (bf16[192,4096]{1,0:T(8,128)(2,1)S(1)}, bf16[192,4096]{1,0:T(8,128)(2,1)}, u32[]{:S(2)}) copy-start(bf16[192,4096]{1,0:T(8,128)(2,1)} %get-tuple-element.17) | copy-start | bytes 4718596

commit v4 on v3

--- a/solution.py
+++ b/solution.py
@@ -162,7 +162,15 @@
         yy = lax.rem(y + step, NY)
         if step > 0:
             entry(yy * 2 + half, step, at(yy, z, core)).start()
-        entry(yy * 2 + 1 - half, NY + step, at(yy, entry_z, core)).start()
+
+    def entry_far(step):
+        yy = lax.rem(y + step, NY)
+        return entry(yy * 2 + 1 - half, NY + step, at(yy, entry_z, core))
+
+    @pl.when(jnp.logical_not(at_end))
+    def _():
+        for step in range(NY):
+            entry_far(step).start()
 
     early = [
         remote(src, dst, early_send.at[i], early_recv.at[i], me, before)
@@ -313,12 +321,18 @@
                 def _():
                     finish(hop * NY + j, j, src_z)
 
+    def pick(values, index, default=0):
+        out = default
+        for i, value in enumerate(values):
+            out = jnp.where(index == i, value, out)
+        return out
+
     def list_at(place, slot):
-        near = jnp.where(slot == 1, place - 1, jnp.where(slot == 5, 1, place + 4 - slot))
-        return jnp.where(place < 2, place + 3 - slot, near)
+        code = pick((0o12, 0o231, 0o3421, 0o145320), place)
+        return lax.rem(code // pick((1, 8, 64, 512, 4096, 32768), slot, 8**6), 8)
 
     def origin(slot):
-        return jnp.where(slot == 1, 1, jnp.where(slot == 5, 2, slot - 4))
+        return pick((9, 1, 0, -2, -1, 2), slot)
 
     flip = last - pos
 
@@ -329,6 +343,8 @@
     def _(it):
         slot_now = it // 2
         part_now = lax.rem(it, 2)
+        from_l = list_at(pos, slot_now)
+        from_r = list_at(flip, slot_now)
 
         for jj in range(2):
             j = 2 * part_now + jj
@@ -339,19 +355,19 @@
                 idx = own_idx(j)
                 arrived(idx)
 
-                @pl.when(pos == 1)
+                @pl.when(pos <= 1)
                 def _():
                     forward(idx, right_sem, right).start()
 
-                @pl.when(pos == 2)
+                @pl.when(pos >= 2)
                 def _():
                     forward(idx, left_sem, left).start()
 
                 share(idx).start()
 
-            @pl.when((slot_now >= 1) & (slot_now <= pos + 2))
-            def _():
-                idx = z_of(-list_at(pos, slot_now)) * NY + src_y
+            @pl.when(from_l > 0)
+            def _():
+                idx = z_of(-from_l) * NY + src_y
                 arrived(idx)
 
                 @pl.when(pos < last)
@@ -360,9 +376,9 @@
 
                 share(idx).start()
 
-            @pl.when((slot_now >= 1) & (slot_now <= flip + 2))
-            def _():
-                idx = z_of(list_at(flip, slot_now)) * NY + src_y
+            @pl.when(from_r > 0)
+            def _():
+                idx = z_of(from_r) * NY + src_y
                 arrived(idx)
 
                 @pl.when(pos > 0)
@@ -371,29 +387,31 @@
 
                 share(idx).start()
 
-        @pl.when(((it == 5) & (pos == 0)) | ((it == 9) & (pos == 2)))
+        @pl.when((it == 1) & at_end)
+        def _():
+            for step in range(NY):
+                entry_far(step).start()
+
+        @pl.when((it == 7) & (pos == 2))
         def _():
             for j in range(NY):
                 forward(own_idx(j), right_sem, right).start()
 
-        @pl.when(((it == 5) & (flip == 0)) | ((it == 9) & (flip == 2)))
+        @pl.when((it == 7) & (pos == 1))
         def _():
             for j in range(NY):
                 forward(own_idx(j), left_sem, left).start()
 
-        @pl.when(it == 2)
+        @pl.when(it == 1)
         def _():
             for copy in w_copies:
                 copy.wait()
 
-        slot_done = slot_now - 1
-        limit = jnp.where(part_now == 0, pos + 2, flip + 2)
-
-        @pl.when((slot_done >= part_now) & (slot_done <= limit) & (slot_done <= 5))
-        def _():
-            place = jnp.where(part_now == 0, pos, flip)
-            away = jnp.where(slot_done == 0, 0, list_at(place, slot_done))
-            compute(z_of(jnp.where(part_now == 0, -away, away)))
+        away = jnp.where(part_now == 0, -list_at(pos, slot_now - 1), list_at(flip, slot_now - 1))
+
+        @pl.when((it == 1) | ((it >= 2) & (away != 0)))
+        def _():
+            compute(z_of(jnp.where(it == 1, 0, away)))
 
         since_l = it - 3 - flip
         slot_l = since_l // 2
@@ -411,7 +429,7 @@
         def _():
             combine(z_of(away_r), away_r, 1)
 
-        @pl.when(it == 14 + lax.rem(pos, 2))
+        @pl.when(it == pick((10, 15, 14, 11), pos))
         def _():
             combine(z, 0, 0)
 

time: 192 us -> 151 us (0.79); the launches traced: 189 us -> 151 us
  Pallas kernels: 166 us -> 128 us
    pallas_call x1, Pallas kernels: 166 us -> 128 us  [experts(): pl.pallas_call(expert_kernel, out_shape=(jax.ShapeDtypeStruct((NY * 2, CA...]
  transfers between devices with their start and end apart: 2 -> 2, of which waited for: 2 -> 1; matrix products, arithmetic and copies ran while one was open for 2% -> 3% of each run, Pallas kernels for 0% -> 0%
where the time goes in v4:
time: 151 us
  Pallas kernels  128 us (85%)
  other arithmetic  10.3 us (7%)
  matrix products  4.32 us (3%)
  local copies, waits for them, and re-layouts  4.28 us (3%)
  starting transfers between devices  2.05 us (1%)
    pallas_call x1, Pallas kernels, experts(): pl.pallas_call(expert_kernel, out_shape=(jax.ShapeDtypeStruct((NY * 2, CA...  128 us
    unnamed x14, local copies, waits for them, and re-layouts  3.71 us
  transfers between devices with their start and end apart: 2, of which 1 were waited for; matrix products, arithmetic and copies ran while one was open for 3% of the time, Pallas kernels for 0%

profile of v4, /device:TPU:25, one launch (start us, length us, event | category | flops | bytes accessed | tf_op | source)
XLA Modules:
  0.0 150.9 jit_solution(2317664523122086801)
XLA Ops:
  0.6 1.5 %fusion = f32[128]{0:T(128)S(1)} fusion(bf16[1,128,4096]{2,1,0:T(8,128)(2,1)} %param.7), kind=kLoop, calls=%fused_computation.7 | loop fusion | flops 1572736 | bytes 1049088 | tf_op jit(solution)/shard_map/reduce_sum | solution.py:586
  2.2 0.7 fusion.13
  2.9 0.7 bitcast_convert_fusion
  3.6 0.7 select_reduce_fusion.2
  4.3 0.1 copy.27
  4.4 0.1 copy.29
  4.5 0.2 reduce_window_sum.11
  4.7 0.0 copy-start
  4.7 1.9 %convolution_convert_fusion.1 = bf16[8,8,4096]{2,1,0:T(8,128)(2,1)S(1)} fusion(f32[4096]{0:T(1024)} %bitcast.60, f32[128]{0:T(128)S(1)} %add_sqrt_fusion.1, s32[8,128]{1,0:T(8,128)S(1)} %copy.28, pred[8,128]{1,0:T(8,128)(4,1)S(1)} %copy.29, bf16[1,128,4096]{2,1,0:T(8,128)(2,1)} %param.7), kind=kOutput, calls=%fused_computation.2 | convolution fusion | flops 69484544 | bytes 1594880 | tf_op jit(solution)/shard_map/wst,td->wsd/dot_general | solution.py:599
  6.6 0.0 copy-done
  6.6 0.3 broadcast_select_fusion.2
  6.9 0.8 collective-permute-start
  7.6 0.1 copy.31
  7.8 0.1 eq.71
  7.8 0.7 fusion.17.place_ref
  8.5 0.7 collective-permute-done
  9.2 0.1 broadcast_select_fusion.1
  9.3 1.0 pad_maximum_fusion.mine_ref
  10.3 128.5 %shard_map.102 = (bf16[8,8,4352]{2,1,0:T(8,128)(2,1)}, bf16[2,192,4096]{2,1,0:T(8,128)(2,1)}, bf16[192,4096]{1,0:T(8,128)(2,1)}, bf16[128,4096]{1,0:T(8,128)(2,1...) custom-call(bf16[8,16,4096]{2,1,0:T(8,128)(2,1)} %pad_maximum_fusion.mine_ref, ...), custom_call_target="tpu_custom_call" | custom-call | tf_op jit(solution)/shard_map/pallas_call | solution.py:522
  138.8 1.5 %fusion.3 = f32[128]{0:T(128)S(1)} fusion(bf16[128,4096]{1,0:T(8,128)(2,1)} %get-tuple-element.15), kind=kLoop, calls=%fused_computation.10 | loop fusion | flops 1572736 | bytes 1049088 | tf_op jit(solution)/shard_map/reduce_sum | solution.py:627
  140.3 0.8 convert_reduce_fusion
  141.1 1.3 collective-permute-start.1
  142.4 0.0 copy-start.1
  142.4 0.0 copy-start.4
  142.4 2.2 %multiply_reduce_fusion = (f32[128]{0:T(128)S(1)}, f32[128,4096]{1,0:T(8,128)S(1)}) fusion(bf16[128,4096]{1,0:T(8,128)(2,1)} %get-tuple-element.15, f32[128]{0:T(128)S(1)} %add_sqrt_fusion, f32[4096]{0:T(1024)} %bitcast.63, bf16[64,128]{1,0:T(8,128)(2,1)} %get-tuple-element.12, bf16[8,8,4352]{2,1,0:T(8,128)(2,1)} %get-tuple-element.13), kind=kOutput, calls=%fused_computation.12 | convolution fusion | flops 69730176 | bytes 3703808 | tf_op jit(solution)/shard_map/dot_general | solution.py:623
  144.6 0.0 copy-done.1
  144.6 0.0 copy-done.4
  144.6 0.0 copy-start.5
  144.6 0.0 copy-start.2
  144.6 1.6 %fusion.9 = bf16[1,128,4096]{2,1,0:T(8,128)(2,1)} fusion(f32[128,4096]{1,0:T(8,128)S(1)} %get-tuple-element.25, f32[128]{0:T(128)S(1)} %broadcast_multiply_fusion, f32[128]{0:T(128)S(1)} %add_sqrt_fusion, bf16[128,4096]{1,0:T(8,128)(2,1)S(1)} %copy-done.1, bf16[128,4096]{1,0:T(8,128)(2,1)S(1)} %copy-done.4), kind=kLoop, calls=%fused_computation.18 | loop fusion | flops 4194304 | bytes 5243904 | tf_op jit(solution)/shard_map/broadcast_in_dim | solution.py:639
  146.3 0.0 collective-permute-done.1
  146.3 0.1 select_reduce_fusion.1
  146.4 0.1 copy.30
  146.5 0.0 copy-done.5
  146.5 0.6 select_reduce_fusion
  147.2 0.0 copy-done.2
  147.2 0.0 copy-start.3
  147.2 1.7 %copy.35 = bf16[1,1,2,192,4096]{4,3,2,1,0:T(8,128)(2,1)} copy(bf16[1,1,2,192,4096]{4,3,2,1,0:T(8,128)(2,1)S(1)} %bitcast.52) | data formatting | bytes 6291456
  148.8 0.9 copy-done.3
  149.7 1.1 copy.36
  (9 shorter events, 0.2 us)
Async XLA Ops:
  4.7 1.9 %copy-start = (bf16[1,128,4096]{2,1,0:T(8,128)(2,1)S(1)}, bf16[1,128,4096]{2,1,0:T(8,128)(2,1)}, u32[]{:S(2)}) copy-start(bf16[1,128,4096]{2,1,0:T(8,128)(2,1)} %param.8) | copy-start | bytes 3145732
  6.9 2.3 %collective-permute-start = (bf16[8,8,4096]{2,1,0:T(8,128)(2,1)S(1)}, bf16[8,8,4096]{2,1,0:T(8,128)(2,1)S(1)}, u32[]{:S(2)}, u32[]{:S(2)}) collective-permute-start(bf16[8,8,4096]{2,1,0:T(8,128)(2,1)S(1)} %get-tuple-element.22), channel_id=1, source_target_pairs={{0,1},{1,0},{2,3},{3,2},{4,5},{5,4},{6,7},{7,6},{8,9},{9,8},{10,11... | collective-permute-start | bytes 1572872 | tf_op jit(solution)/shard_map/ppermute | solution.py:603
  141.1 5.1 %collective-permute-start.1 = (f32[8,8]{1,0:T(8,128)S(1)}, f32[8,8]{1,0:T(8,128)S(1)}, u32[]{:S(2)}, u32[]{:S(2)}) collective-permute-start(f32[8,8]{1,0:T(8,128)S(1)} %convert_reduce_fusion), channel_id=1, source_target_pairs={{0,64},{64,128},{128,192},{192,0},{1,65},{65,129},{129,193},{193,1... | collective-permute-start | bytes 776 | tf_op jit(solution)/shard_map/ppermute | solution.py:619
  142.4 2.2 %copy-start.1 = (bf16[128,4096]{1,0:T(8,128)(2,1)S(1)}, bf16[128,4096]{1,0:T(8,128)(2,1)}, u32[]{:S(2)}) copy-start(bf16[128,4096]{1,0:T(8,128)(2,1)} %get-tuple-element.15) | copy-start | bytes 3145732
  142.4 2.2 %copy-start.4 = (bf16[128,4096]{1,0:T(8,128)(2,1)S(1)}, bf16[128,4096]{1,0:T(8,128)(2,1)}, u32[]{:S(2)}) copy-start(bf16[128,4096]{1,0:T(8,128)(2,1)} %get-tuple-element.11) | copy-start | bytes 3145732
  144.6 1.9 %copy-start.5 = (s32[1,128,8]{1,2,0:T(8,128)S(1)}, s32[1,128,8]{1,2,0:T(8,128)}, u32[]{:S(2)}) copy-start(s32[1,128,8]{1,2,0:T(8,128)} %param.9) | copy-start | bytes 12292
  144.6 2.5 %copy-start.2 = (bf16[2,192,4096]{2,1,0:T(8,128)(2,1)S(1)}, bf16[2,192,4096]{2,1,0:T(8,128)(2,1)}, u32[]{:S(2)}) copy-start(bf16[2,192,4096]{2,1,0:T(8,128)(2,1)} %get-tuple-element.16) | copy-start | bytes 9437188
  147.2 2.5 %copy-start.3 = (bf16[192,4096]{1,0:T(8,128)(2,1)S(1)}, bf16[192,4096]{1,0:T(8,128)(2,1)}, u32[]{:S(2)}) copy-start(bf16[192,4096]{1,0:T(8,128)(2,1)} %get-tuple-element.17) | copy-start | bytes 4718596

commit v5 on v4

--- a/solution.py
+++ b/solution.py
@@ -36,6 +36,7 @@
     gain_ref,
     place_ref,
     back_ref,
+    dc_ref,
     ggu_hbm,
     gd_hbm,
     hidden_next,
@@ -68,6 +69,8 @@
     chain_recv,
     final_send,
     back_recv,
+    dc_send,
+    dc_recv,
     w_sem,
     out_sem,
     early_send,
@@ -129,6 +132,12 @@
         for yy in range(NY):
             greet(after, at(yy, z, cc))
             greet(after, at(yy, entry_z, cc))
+    for yy in range(NY):
+        greet(stage, at(yy, entry_z, 0))
+
+        @pl.when((yy != y) | (core != 0))
+        def _():
+            greet(stage, at(yy, z, 0))
 
     w_copies = [
         pltpu.make_async_copy(wgu_hbm, wgu, w_sem.at[0]),
@@ -136,8 +145,9 @@
     ]
     for copy in w_copies:
         copy.start()
-    common = 1 + (NY - 1) + NY + 2 * NY
-    pl.semaphore_wait(barrier, jnp.where(at_end, common + 1 + 4 * NY, common + 2))
+    common = 1 + (NY - 1) + NY + 2 * NY + jnp.where(core == 0, 2 * NY - 1, 0)
+    ends = 1 + 4 * NY + jnp.where(core == 0, 4 * NY, 0)
+    pl.semaphore_wait(barrier, common + jnp.where(at_end, ends, 2))
 
     def remote(src, dst, send, recv, other, pipe=None):
         return pltpu.make_async_remote_copy(
@@ -243,14 +253,16 @@
         part[span, :, :128] = dc
         part[span, :, width + 128 :] = dc
         tile = 512
-        for n in range(width // tile):
-            du = nn(dga, wgu[0, :, n * tile : (n + 1) * tile]) + nn(
-                dgb, wgu[1, :, n * tile : (n + 1) * tile]
-            )
-            part[span, :, 128 + n * tile : 128 + (n + 1) * tile] = du.astype(BF16).reshape(
-                NY, 16, tile
-            )
-        swap_copy(src_z).start()
+        for turn in range(2):
+            low = (1 - core if turn == 0 else core) * halfw
+            for n in range(halfw // tile):
+                cols = pl.ds(pl.multiple_of(low + n * tile, tile), tile)
+                du = nn(dga, wgu[0, :, cols]) + nn(dgb, wgu[1, :, cols])
+                part[span, :, pl.ds(pl.multiple_of(128 + low + n * tile, 128), tile)] = (
+                    du.astype(BF16).reshape(NY, 16, tile)
+                )
+            if turn == 0:
+                swap_copy(src_z).start()
 
     def chain_in(idx):
         pltpu.make_async_copy(summed.at[0], chain.at[idx], chain_recv.at[idx]).wait()
@@ -269,10 +281,36 @@
             before,
         )
 
+    def dc_out(number, cc, src_y, src_z):
+        return remote(
+            final.at[number, pl.ds(cc * CAP, CAP), pl.ds(0, 128)],
+            dc_ref.at[expert],
+            dc_send.at[2 * number + cc],
+            dc_recv.at[expert],
+            at(src_y, src_z, cc),
+        )
+
+    def dc_own(number):
+        return pltpu.make_async_copy(
+            final.at[number, pl.ds(0, CAP), pl.ds(0, 128)], dc_ref.at[expert], dc_recv.at[expert]
+        )
+
     def finish(number, src_y, src_z):
         final[number] = acc[...].astype(BF16)
         for cc in range(2):
             final_out(number, cc, src_y, src_z).start()
+
+        @pl.when(core == 0)
+        def _():
+            dc_out(number, 1, src_y, src_z).start()
+
+            @pl.when((src_y == y) & (src_z == z))
+            def _():
+                dc_own(number).start()
+
+            @pl.when((src_y != y) | (src_z != z))
+            def _():
+                dc_out(number, 0, src_y, src_z).start()
 
     def combine(src_z, hop, kind):
         swap_copy(src_z).wait_recv()
@@ -339,7 +377,7 @@
     def own_idx(j):
         return z * NY + lax.rem(y + NY - j, NY)
 
-    @pl.loop(0, 16)
+    @pl.loop(0, 15)
     def _(it):
         slot_now = it // 2
         part_now = lax.rem(it, 2)
@@ -407,7 +445,14 @@
             for copy in w_copies:
                 copy.wait()
 
-        away = jnp.where(part_now == 0, -list_at(pos, slot_now - 1), list_at(flip, slot_now - 1))
+        gone_l = list_at(pos, slot_now - 1)
+        gone_r = list_at(flip, slot_now - 1)
+        late = slot_now >= 4
+        away = jnp.where(
+            part_now == 0,
+            jnp.where(late & (gone_r > 0), gone_r, -gone_l),
+            jnp.where(late, 0, gone_r),
+        )
 
         @pl.when((it == 1) | ((it >= 2) & (away != 0)))
         def _():
@@ -421,21 +466,26 @@
         def _():
             combine(z_of(-away_l), away_l, -1)
 
-        since_r = it - 4 - pos
-        slot_r = since_r // 2
+        since_r = it - 3 - pos
+        slot_r = (since_r + 16) // 2 - 8
         away_r = flip - origin(slot_r)
-
-        @pl.when((since_r >= 2) & (lax.rem(since_r + 2, 2) == 0) & (slot_r <= 5) & (away_r >= 1))
+        odd_r = lax.rem(since_r + 16, 2)
+
+        @pl.when(
+            (slot_r >= jnp.where(odd_r == 1, 1, 3))
+            & (slot_r <= jnp.where(odd_r == 1, 2, 5))
+            & (away_r >= 1)
+        )
         def _():
             combine(z_of(away_r), away_r, 1)
 
-        @pl.when(it == pick((10, 15, 14, 11), pos))
+        @pl.when(it == pick((10, 14, 14, 11), pos))
         def _():
             combine(z, 0, 0)
 
-        @pl.loop(0, 3)
+        @pl.loop(0, 4)
         def _(s):
-            n = 3 * (it - 13) - 1 + s
+            n = 4 * (it - 13) + s
             tile = 512
 
             @pl.when((n >= 0) & (n < width // tile))
@@ -490,6 +540,14 @@
             def _():
                 for cc in range(2):
                     final_out(hop * NY + j, cc, j, z).wait_send()
+
+                @pl.when(core == 0)
+                def _():
+                    dc_out(hop * NY + j, 1, j, z).wait_send()
+
+                    @pl.when((hop > 0) | (j != y))
+                    def _():
+                        dc_out(hop * NY + j, 0, j, z).wait_send()
 
     @pl.loop(0, slots)
     def _(idx):
@@ -506,6 +564,9 @@
                 back_ref.at[e, :, pl.ds(cc * outw, outw)],
                 back_recv.at[2 * e + cc],
             ).wait()
+        pltpu.make_async_copy(
+            final.at[0, pl.ds(0, CAP), pl.ds(0, 128)], dc_ref.at[e], dc_recv.at[e]
+        ).wait()
     for copy in out_copies:
         copy.wait()
 
@@ -523,6 +584,7 @@
         expert_kernel,
         out_shape=(
             jax.ShapeDtypeStruct((NY * 2, CAP, 2 * outw), BF16),
+            jax.ShapeDtypeStruct((NY * 2, CAP, 128), BF16),
             like(wgu),
             like(wd),
             like(hidden),
@@ -531,7 +593,7 @@
             like(place),
         ),
         in_specs=[vmem] + [hbm] * 6,
-        out_specs=[vmem] + [hbm] * 6,
+        out_specs=[vmem, vmem] + [hbm] * 6,
         scratch_shapes=[
             pltpu.VMEM((2, slots, 16, width), BF16),
             pltpu.VMEM(wgu.shape, BF16),
@@ -559,6 +621,8 @@
             dma((slots + NY,)),
             dma((6 * NY,)),
             dma((4 * NY,)),
+            dma((6 * NY,)),
+            dma((2 * NY,)),
             dma((2,)),
             dma((2,)),
             dma((4,)),
@@ -568,6 +632,106 @@
             collective_id=0, has_side_effects=True, vmem_limit_bytes=60 * 1024 * 1024
         ),
     )(mine, wgu, wd, hidden, grad, gain, place)
+
+
+def finish_kernel(
+    back_hbm,
+    hidden_hbm,
+    grad_hbm,
+    place_ref,
+    gain_ref,
+    ggu_hbm,
+    gd_hbm,
+    handed_hbm,
+    ggu_out,
+    gd_out,
+    back,
+    hidden,
+    grad,
+    handed,
+    ggu,
+    gd,
+    scaled,
+    in_sem,
+    out_sem,
+):
+    width = hidden.shape[1]
+    count = hidden.shape[0]
+    ins = [
+        pltpu.make_async_copy(src, dst, in_sem.at[i])
+        for i, (src, dst) in enumerate(
+            (
+                (hidden_hbm, hidden),
+                (back_hbm, back),
+                (grad_hbm, grad),
+                (ggu_hbm, ggu),
+                (gd_hbm, gd),
+            )
+        )
+    ]
+    for copy in ins:
+        copy.start()
+    ins[0].wait()
+    tile = 512
+    square = jnp.zeros((count, 128), F32)
+    for n in range(width // 128):
+        h = hidden[:, n * 128 : (n + 1) * 128].astype(F32)
+        square = square + h * h
+    rms = jnp.sqrt(jnp.sum(square, axis=1, keepdims=True) / width + 1e-06)
+    ins[1].wait()
+    place = place_ref[...]
+    along = jnp.zeros((count, 1), F32)
+    for n in range(width // tile):
+        cols = slice(n * tile, (n + 1) * tile)
+        rows = back[:, :, 128 + n * tile : 128 + (n + 1) * tile].reshape(-1, tile)
+        part = tn(place, rows) * gain_ref[:, cols]
+        scaled[:, cols] = part
+        along = along + jnp.sum(part * (hidden[:, cols].astype(F32) / rms), axis=1, keepdims=True)
+    inner = along / width
+    for i in (3, 4):
+        ins[i].wait()
+    outs = [
+        pltpu.make_async_copy(ggu, ggu_out, out_sem.at[0]),
+        pltpu.make_async_copy(gd, gd_out, out_sem.at[1]),
+        pltpu.make_async_copy(handed, handed_hbm, out_sem.at[2]),
+    ]
+    outs[0].start()
+    outs[1].start()
+    ins[2].wait()
+    for n in range(width // tile):
+        cols = slice(n * tile, (n + 1) * tile)
+        normed = hidden[:, cols].astype(F32) / rms
+        handed[:, cols] = (
+            grad[:, cols].astype(F32) + (scaled[:, cols] - normed * inner) / rms
+        ).astype(BF16)
+    outs[2].start()
+    for copy in outs:
+        copy.wait()
+
+
+def finish(back, hidden, grad, place, gain, ggu, gd):
+    like = lambda array: jax.ShapeDtypeStruct(array.shape, array.dtype)
+    hbm = pl.BlockSpec(memory_space=pl.ANY)
+    vmem = pl.BlockSpec(memory_space=pltpu.VMEM)
+    room = lambda array: pltpu.VMEM(array.shape, array.dtype)
+    return pl.pallas_call(
+        finish_kernel,
+        out_shape=(like(hidden), like(ggu), like(gd)),
+        in_specs=[hbm, hbm, hbm, vmem, vmem, hbm, hbm],
+        out_specs=[hbm, hbm, hbm],
+        scratch_shapes=[
+            room(back),
+            room(hidden),
+            room(grad),
+            room(hidden),
+            room(ggu),
+            room(gd),
+            pltpu.VMEM(hidden.shape, F32),
+            pltpu.SemaphoreType.DMA((5,)),
+            pltpu.SemaphoreType.DMA((3,)),
+        ],
+        compiler_params=pltpu.CompilerParams(vmem_limit_bytes=48 * 1024 * 1024),
+    )(back, hidden, grad, place, gain, ggu, gd)
 
 
 def on_device(hidden_in, out_grad, expert_ids, route_weight, norm_gain, w_gate_up, w_down):
@@ -605,7 +769,7 @@
     second = jnp.where(core == 0, got, keep)
     mine = jnp.concatenate([first, second], axis=1)
 
-    back, grad_gate_up, grad_down, hidden_next, grad_next, gain_next, place_next = experts(
+    back, dc_back, ggu, gd, hidden_next, grad_next, gain_next, place_next = experts(
         mine,
         w_gate_up[0, 0],
         w_down[0, 0],
@@ -615,23 +779,11 @@
         place_bf.reshape(span * CAP, -1),
     )
 
-    stages = lax.axis_size("pipe")
-    comb_rows = lax.ppermute(
-        back[:, :, 0].astype(F32), "pipe", [(i, (i + 1) % stages) for i in range(stages)]
+    handed, grad_gate_up, grad_down = finish(
+        back, hidden_next, grad_next, place_next, gain_next.reshape(1, width), ggu, gd
     )
-    summed_in = back[:, :, 128 : width + 128].reshape(span * CAP, width)
-    grad_normed = lax.dot_general(
-        place_next, summed_in, (((0,), (0,)), ((), ())), preferred_element_type=F32
-    )
-    next_f = hidden_next.astype(F32)
-    next_rms = jnp.sqrt(jnp.mean(next_f * next_f, axis=-1, keepdims=True) + 1e-06)
-    next_normed = next_f / next_rms
-    scaled = grad_normed * gain_next.reshape(width)
-    inner_mean = jnp.mean(scaled * next_normed, axis=-1, keepdims=True)
-    handed = (
-        grad_next.astype(F32) + (scaled - next_normed * inner_mean) / next_rms
-    ).astype(BF16)
-
+
+    comb_rows = dc_back[:, :, 0].astype(F32)
     comb_te = jnp.sum(place_f * comb_rows[:, :, None], axis=1)
     comb_te = comb_te / jnp.where(member.T == 1, weight_te.T, 1.0)
     grad_combine = jnp.sum(jnp.where(picked, comb_te.T[:, None, :], 0.0), axis=-1)

time: 151 us -> 146 us (0.967)
  other arithmetic: 10.3 us -> 7.19 us
  local copies, waits for them, and re-layouts: 4.28 us -> 6.94 us
  matrix products: 4.32 us -> 2.12 us
    pallas_call x1, Pallas kernels: 128 us -> 122 us  [experts(): pl.pallas_call(expert_kernel, out_shape=(jax.ShapeDtypeStruct((NY * 2, CA...]
    pallas_call x0 -> x1, Pallas kernels: none -> 4.7 us  [finish(): pl.pallas_call(finish_kernel, out_shape=(like(hidden), like(ggu), like(gd...]
    unnamed x14 -> x16, local copies, waits for them, and re-layouts: 3.71 us -> 6.35 us
    dot_general x1 -> x0, matrix products: 2.17 us -> none  [on_device(): lax.dot_general(place_next, summed_in, (((0,), (0,)), ((), ())), preferre...]
    broadcast_in_dim x1 -> x0, other arithmetic: 1.62 us -> none  [on_device(): handed[None]]
    reduce_sum x1 -> x0, other arithmetic: 1.52 us -> none  [on_device(): jnp.mean(next_f * next_f, axis=-1, keepdims=True) + 1e-06]
  transfers between devices with their start and end apart: 2 -> 1, of which waited for: 1 -> 1; matrix products, arithmetic and copies ran while one was open for 3% -> 1% of each run, Pallas kernels for 0% -> 0%
where the time goes in v5:
time: 146 us; the launch traced here: 145 us
  Pallas kernels  127 us (87%)
  other arithmetic  7.19 us (5%)
  local copies, waits for them, and re-layouts  6.94 us (5%)
  matrix products  2.12 us (1%)
    pallas_call x1, Pallas kernels, experts(): pl.pallas_call(expert_kernel, out_shape=(jax.ShapeDtypeStruct((NY * 2, CA...  122 us
    unnamed x16, local copies, waits for them, and re-layouts  6.35 us
    pallas_call x1, Pallas kernels, finish(): pl.pallas_call(finish_kernel, out_shape=(like(hidden), like(ggu), like(gd...  4.7 us
  transfers between devices with their start and end apart: 1, of which 1 were waited for; matrix products, arithmetic and copies ran while one was open for 1% of the time, Pallas kernels for 0%

profile of v5, /device:TPU:25, one launch (start us, length us, event | category | flops | bytes accessed | tf_op | source)
XLA Modules:
  0.0 145.3 jit_solution(16009018774794044733)
XLA Ops:
  0.6 0.7 fusion.9
  1.3 0.1 copy.27
  1.5 0.2 reduce_window_sum.11
  1.7 0.1 copy.29
  1.8 1.5 %fusion = f32[128]{0:T(128)S(1)} fusion(bf16[1,128,4096]{2,1,0:T(8,128)(2,1)} %param.7), kind=kLoop, calls=%fused_computation.4 | loop fusion | flops 1572736 | bytes 1049088 | tf_op jit(solution)/shard_map/reduce_sum | solution.py:750
  3.4 0.7 bitcast_convert_fusion
  4.0 0.7 select_reduce_fusion.2
  4.7 0.0 copy-start.6
  4.7 1.8 %convolution_convert_fusion.1 = bf16[8,8,4096]{2,1,0:T(8,128)(2,1)S(1)} fusion(f32[4096]{0:T(1024)} %bitcast.52, f32[128]{0:T(128)S(1)} %add_sqrt_fusion, s32[8,128]{1,0:T(8,128)S(1)} %copy.28, pred[8,128]{1,0:T(8,128)(4,1)S(1)} %copy.29, bf16[1,128,4096]{2,1,0:T(8,128)(2,1)} %param.7), kind=kOutput, calls=%fused_computation.1 | convolution fusion | flops 69484544 | bytes 1594880 | tf_op jit(solution)/shard_map/wst,td->wsd/dot_general | solution.py:763
  6.6 0.0 copy-done.6
  6.6 0.3 broadcast_select_fusion.2
  6.9 0.8 collective-permute-start
  7.7 0.1 copy.31
  7.8 0.1 eq.71
  7.8 0.7 fusion.13.place_ref
  8.5 0.7 collective-permute-done
  9.2 0.1 broadcast_select_fusion.1
  9.3 1.0 pad_maximum_fusion.mine_ref
  10.3 0.0 copy-start.7
  10.3 122.3 %shard_map.102 = (bf16[8,8,4352]{2,1,0:T(8,128)(2,1)}, bf16[8,8,128]{2,1,0:T(8,128)(2,1)}, bf16[2,192,4096]{2,1,0:T(8,128)(2,1)}, bf16[192,4096]{1,0:T(8,128)(2,...) custom-call(bf16[8,16,4096]{2,1,0:T(8,128)(2,1)} %pad_maximum_fusion.mi, ...), custom_call_target="tpu_custom_call" | custom-call | tf_op jit(solution)/shard_map/pallas_call | solution.py:583
  132.6 0.8 convert_reduce_fusion
  133.4 0.1 select_reduce_fusion.1
  133.5 0.1 copy.30
  133.7 0.0 copy-done.7
  133.7 0.6 select_reduce_fusion
  134.3 0.0 copy-start
  134.3 1.4 copy-done
  135.7 0.0 copy-start.1
  135.7 1.2 copy-done.1
  136.9 0.0 copy-start.2
  136.9 1.2 copy-done.2
  138.2 0.0 copy-start.3
  138.2 1.1 copy-done.3
  139.2 0.0 copy-start.4
  139.2 0.7 copy-done.4
  139.9 0.0 copy-start.5
  139.9 0.7 copy-done.5
  140.7 4.7 %shard_map.103 = (bf16[128,4096]{1,0:T(8,128)(2,1)}, bf16[2,192,4096]{2,1,0:T(8,128)(2,1)}, bf16[192,4096]{1,0:T(8,128)(2,1)}) custom-call(bf16[8,8,4352]{2,1,0:T(8,128)(2,1)S(1)} %copy-done.3, bf16[128,4096]{1,0:T(8,128)(2,1)S(1)} %copy-done.1, bf16[128,4096]{1,0:T(8,128)(2,1)S(1)} %copy-done.2, bf16[64,128]{1,0:T(8,128)(2,1)S(1)} %copy-done.5, ...), custom_call_target="tpu_custom_call" | custom-call | tf_op jit(solution)/shard_map/pallas_call | solution.py:717
  (7 shorter events, 0.2 us)
Async XLA Ops:
  4.7 1.8 %copy-start.6 = (bf16[1,128,4096]{2,1,0:T(8,128)(2,1)S(1)}, bf16[1,128,4096]{2,1,0:T(8,128)(2,1)}, u32[]{:S(2)}) copy-start(bf16[1,128,4096]{2,1,0:T(8,128)(2,1)} %param.8) | copy-start | bytes 3145732
  6.9 2.3 %collective-permute-start = (bf16[8,8,4096]{2,1,0:T(8,128)(2,1)S(1)}, bf16[8,8,4096]{2,1,0:T(8,128)(2,1)S(1)}, u32[]{:S(2)}, u32[]{:S(2)}) collective-permute-start(bf16[8,8,4096]{2,1,0:T(8,128)(2,1)S(1)} %get-tuple-element.30), channel_id=1, source_target_pairs={{0,1},{1,0},{2,3},{3,2},{4,5},{5,4},{6,7},{7,6},{8,9},{9,8},{10,11... | collective-permute-start | bytes 1572872 | tf_op jit(solution)/shard_map/ppermute | solution.py:767
  10.3 123.3 %copy-start.7 = (s32[1,128,8]{1,2,0:T(8,128)S(1)}, s32[1,128,8]{1,2,0:T(8,128)}, u32[]{:S(2)}) copy-start(s32[1,128,8]{1,2,0:T(8,128)} %param.9) | copy-start | bytes 12292
  134.3 1.4 copy-start
  135.7 1.2 copy-start.1
  136.9 1.2 copy-start.2
  138.2 1.1 copy-start.3
  139.2 0.7 copy-start.4
  139.9 0.7 copy-start.5

commit v6 on v5

--- a/solution.py
+++ b/solution.py
@@ -430,14 +430,19 @@
             for step in range(NY):
                 entry_far(step).start()
 
-        @pl.when((it == 7) & (pos == 2))
-        def _():
-            for j in range(NY):
+        first = jnp.where(it == 1, 0, 3)
+        until = jnp.where(it == 1, 3, NY)
+
+        @pl.when(((it == 1) | (it == 7)) & (pos == 2))
+        def _():
+            @pl.loop(first, until)
+            def _(j):
                 forward(own_idx(j), right_sem, right).start()
 
-        @pl.when((it == 7) & (pos == 1))
-        def _():
-            for j in range(NY):
+        @pl.when(((it == 1) | (it == 7)) & (pos == 1))
+        def _():
+            @pl.loop(first, until)
+            def _(j):
                 forward(own_idx(j), left_sem, left).start()
 
         @pl.when(it == 1)
@@ -730,7 +735,7 @@
             pltpu.SemaphoreType.DMA((5,)),
             pltpu.SemaphoreType.DMA((3,)),
         ],
-        compiler_params=pltpu.CompilerParams(vmem_limit_bytes=48 * 1024 * 1024),
+        compiler_params=pltpu.CompilerParams(vmem_limit_bytes=63 * 1024 * 1024),
     )(back, hidden, grad, place, gain, ggu, gd)
 
 

time: 146 us -> 140 us (0.959)
  local copies, waits for them, and re-layouts: 6.94 us -> 0.6 us
    unnamed x16 -> x4, local copies, waits for them, and re-layouts: 6.35 us -> 0.01 us
    pallas_call x1, Pallas kernels: 4.7 us -> 6.46 us  [finish(): pl.pallas_call(finish_kernel, out_shape=(like(hidden), like(ggu), like(gd...]
where the time goes in v6:
time: 140 us
  Pallas kernels  128 us (91%)
  other arithmetic  7.19 us (5%)
  matrix products  2.12 us (2%)
    pallas_call x1, Pallas kernels, experts(): pl.pallas_call(expert_kernel, out_shape=(jax.ShapeDtypeStruct((NY * 2, CA...  121 us
    pallas_call x1, Pallas kernels, finish(): pl.pallas_call(finish_kernel, out_shape=(like(hidden), like(ggu), like(gd...  6.46 us
  transfers between devices with their start and end apart: 1, of which 1 were waited for; matrix products, arithmetic and copies ran while one was open for 1% of the time, Pallas kernels for 0%

profile of v6, /device:TPU:25, one launch (start us, length us, event | category | flops | bytes accessed | tf_op | source)
XLA Modules:
  0.0 139.8 jit_solution(5536835930973212780)
XLA Ops:
  0.6 0.7 fusion.9
  1.3 0.1 copy.27
  1.5 0.2 reduce_window_sum.11
  1.7 0.1 copy.29
  1.8 1.5 %fusion = f32[128]{0:T(128)S(1)} fusion(bf16[1,128,4096]{2,1,0:T(8,128)(2,1)} %param.7), kind=kLoop, calls=%fused_computation.4 | loop fusion | flops 1572736 | bytes 1049088 | tf_op jit(solution)/shard_map/reduce_sum | solution.py:755
  3.4 0.7 bitcast_convert_fusion
  4.0 0.7 select_reduce_fusion.2
  4.7 0.0 copy-start
  4.7 1.8 %convolution_convert_fusion.1 = bf16[8,8,4096]{2,1,0:T(8,128)(2,1)S(1)} fusion(f32[4096]{0:T(1024)} %bitcast.51, f32[128]{0:T(128)S(1)} %add_sqrt_fusion, s32[8,128]{1,0:T(8,128)S(1)} %copy.28, pred[8,128]{1,0:T(8,128)(4,1)S(1)} %copy.29, bf16[1,128,4096]{2,1,0:T(8,128)(2,1)} %param.7), kind=kOutput, calls=%fused_computation.1 | convolution fusion | flops 69484544 | bytes 1594880 | tf_op jit(solution)/shard_map/wst,td->wsd/dot_general | solution.py:768
  6.6 0.0 copy-done
  6.6 0.3 broadcast_select_fusion.2
  6.9 0.8 collective-permute-start
  7.7 0.1 copy.31
  7.8 0.1 eq.71
  7.8 0.7 fusion.13.place_ref
  8.5 0.7 collective-permute-done
  9.2 0.1 broadcast_select_fusion.1
  9.3 1.0 pad_maximum_fusion.mine_ref
  10.3 0.0 copy-start.1
  10.3 121.3 %shard_map.102 = (bf16[8,8,4352]{2,1,0:T(8,128)(2,1)}, bf16[8,8,128]{2,1,0:T(8,128)(2,1)}, bf16[2,192,4096]{2,1,0:T(8,128)(2,1)}, bf16[192,4096]{1,0:T(8,128)(2,...) custom-call(bf16[8,16,4096]{2,1,0:T(8,128)(2,1)} %pad_maximum_fusion.mi, ...), custom_call_target="tpu_custom_call" | custom-call | tf_op jit(solution)/shard_map/pallas_call | solution.py:588
  131.7 0.8 convert_reduce_fusion
  132.5 0.1 select_reduce_fusion.1
  132.5 0.1 copy.30
  132.7 0.0 copy-done.1
  132.7 0.6 select_reduce_fusion
  133.3 6.5 %shard_map.103 = (bf16[128,4096]{1,0:T(8,128)(2,1)}, bf16[2,192,4096]{2,1,0:T(8,128)(2,1)}, bf16[192,4096]{1,0:T(8,128)(2,1)}) custom-call(bf16[8,8,4352]{2,1,0:T(8,128)(2,1)} %get-tuple-element.15.back_hbm, bf16[128,4096]{1,0:T(8,128)(2,1)} %get-tuple-element.16.hidden_hbm, bf16[128,4096]{1,0:T(8,128)(2,1)} %get-tuple-element.17.grad_hbm, ...), custom_call_target="tpu_custom_call" | custom-call | tf_op jit(solution)/shard_map/pallas_call | solution.py:722
  (7 shorter events, 0.2 us)
Async XLA Ops:
  4.7 1.8 %copy-start = (bf16[1,128,4096]{2,1,0:T(8,128)(2,1)S(1)}, bf16[1,128,4096]{2,1,0:T(8,128)(2,1)}, u32[]{:S(2)}) copy-start(bf16[1,128,4096]{2,1,0:T(8,128)(2,1)} %param.8) | copy-start | bytes 3145732
  6.9 2.3 %collective-permute-start = (bf16[8,8,4096]{2,1,0:T(8,128)(2,1)S(1)}, bf16[8,8,4096]{2,1,0:T(8,128)(2,1)S(1)}, u32[]{:S(2)}, u32[]{:S(2)}) collective-permute-start(bf16[8,8,4096]{2,1,0:T(8,128)(2,1)S(1)} %get-tuple-element.30), channel_id=1, source_target_pairs={{0,1},{1,0},{2,3},{3,2},{4,5},{5,4},{6,7},{7,6},{8,9},{9,8},{10,11... | collective-permute-start | bytes 1572872 | tf_op jit(solution)/shard_map/ppermute | solution.py:772
  10.3 122.4 %copy-start.1 = (s32[1,128,8]{1,2,0:T(8,128)S(1)}, s32[1,128,8]{1,2,0:T(8,128)}, u32[]{:S(2)}) copy-start(s32[1,128,8]{1,2,0:T(8,128)} %param.9) | copy-start | bytes 12292

commit v7 on v6

--- a/solution.py
+++ b/solution.py
@@ -5,7 +5,6 @@
 from jax.experimental.pallas import tpu as pltpu
 from jax.sharding import PartitionSpec as P
 
-SPLIT = 8
 CAP = 8
 NY = 4
 NZ = 8
@@ -27,14 +26,38 @@
     return lax.dot_general(left, right, (((0,), (0,)), ((), ())), preferred_element_type=F32)
 
 
+def placing(ids, weights):
+    count = ids.shape[1]
+    span = NY * 2
+    hits = [ids == e for e in range(span)]
+    member = jnp.concatenate(
+        [jnp.max(jnp.where(hit, 1.0, 0.0), axis=0, keepdims=True) for hit in hits], axis=0
+    )
+    above = lax.broadcasted_iota(jnp.int32, (count, count), 0) < lax.broadcasted_iota(
+        jnp.int32, (count, count), 1
+    )
+    position = nn(member.astype(BF16), jnp.where(above, 1.0, 0.0).astype(BF16))
+    row = lax.broadcasted_iota(jnp.int32, (CAP, count), 0).astype(F32)
+    plain = []
+    weighted = []
+    for e in range(span):
+        here = (row == position[e : e + 1]) & (member[e : e + 1] > 0.5)
+        place = jnp.where(here, 1.0, 0.0)
+        share = jnp.sum(jnp.where(hits[e], weights, 0.0), axis=0, keepdims=True)
+        plain.append(place)
+        weighted.append(place * share)
+    return plain, weighted
+
+
 def expert_kernel(
-    mine_ref,
+    ids_ref,
+    weight_ref,
+    gain_row,
     wgu_hbm,
     wd_hbm,
     hidden_ref,
     grad_ref,
     gain_ref,
-    place_ref,
     back_ref,
     dc_ref,
     ggu_hbm,
@@ -43,6 +66,11 @@
     grad_next,
     gain_next,
     place_next,
+    mine_ref,
+    give,
+    place_ref,
+    tokens,
+    token_grad,
     rows,
     wgu,
     wd,
@@ -75,6 +103,9 @@
     out_sem,
     early_send,
     early_recv,
+    pack_sem,
+    give_send,
+    give_recv,
 ):
     me = lax.axis_index("expert")
     stage = lax.axis_index("pipe")
@@ -102,6 +133,13 @@
     left = at(y, lax.rem(z + NZ - 1, NZ), core)
     entry_z = jnp.where(pos >= 2, lax.rem(LINE * (half + 1), NZ), lax.rem(LINE * half + NZ - 1, NZ))
 
+    loads = [
+        pltpu.make_async_copy(hidden_ref, tokens, pack_sem.at[0]),
+        pltpu.make_async_copy(grad_ref, token_grad, pack_sem.at[1]),
+    ]
+    for copy in loads:
+        copy.start()
+
     barrier = pltpu.get_barrier_semaphore()
 
     def greet(pipe, other):
@@ -145,6 +183,35 @@
     ]
     for copy in w_copies:
         copy.start()
+
+    plain, weighted = placing(ids_ref[...], weight_ref[...].astype(F32))
+    place = jnp.concatenate(plain, axis=0).astype(BF16)
+    place_w = jnp.concatenate(weighted, axis=0).astype(BF16)
+    place_ref[...] = place
+    for copy in loads:
+        copy.wait()
+    count = tokens.shape[0]
+    square = jnp.zeros((count, 128), F32)
+    for n in range(width // 128):
+        h = tokens[:, n * 128 : (n + 1) * 128].astype(F32)
+        square = square + h * h
+    rms = jnp.sqrt(jnp.sum(square, axis=1, keepdims=True) / width + 1e-06)
+    for n in range(width // 512):
+        cols = slice(n * 512, (n + 1) * 512)
+        u = ((tokens[:, cols].astype(F32) / rms) * gain_row[:, cols]).astype(BF16)
+        sent_in = nn(place, u).astype(BF16).reshape(NY * 2, CAP, 512)
+        sent_grad = nn(place_w, token_grad[:, cols]).astype(BF16).reshape(NY * 2, CAP, 512)
+
+        @pl.when(core == 0)
+        def _():
+            mine_ref[:, :CAP, cols] = sent_in
+            give[:, :, cols] = sent_grad
+
+        @pl.when(core == 1)
+        def _():
+            mine_ref[:, CAP:, cols] = sent_grad
+            give[:, :, cols] = sent_in
+
     common = 1 + (NY - 1) + NY + 2 * NY + jnp.where(core == 0, 2 * NY - 1, 0)
     ends = 1 + 4 * NY + jnp.where(core == 0, 4 * NY, 0)
     pl.semaphore_wait(barrier, common + jnp.where(at_end, ends, 2))
@@ -158,6 +225,21 @@
             device_id={"pipe": stage if pipe is None else pipe, "expert": other},
             device_id_type=MESH,
         )
+
+    def give_copy(place_of):
+        return remote(
+            give, mine_ref.at[:, pl.ds(place_of * CAP, CAP)], give_send.at[0], give_recv.at[0], partner
+        )
+
+    @pl.when(core == 0)
+    def _():
+        give_copy(0).start()
+
+    @pl.when(core == 1)
+    def _():
+        give_copy(1).start()
+
+    give_copy(0).wait()
 
     slot = z * NY + y
 
@@ -576,8 +658,9 @@
         copy.wait()
 
 
-def experts(mine, wgu, wd, hidden, grad, gain, place):
-    width = mine.shape[2]
+def experts(ids, weights, gain_row, wgu, wd, hidden, grad, gain):
+    width = hidden.shape[1]
+    count = hidden.shape[0]
     units = wd.shape[0]
     outw = width // 2 + 128
     slots = NY * NZ
@@ -595,11 +678,16 @@
             like(hidden),
             like(grad),
             like(gain),
-            like(place),
+            jax.ShapeDtypeStruct((NY * 2 * CAP, count), BF16),
         ),
-        in_specs=[vmem] + [hbm] * 6,
+        in_specs=[vmem] * 3 + [hbm] * 5,
         out_specs=[vmem, vmem] + [hbm] * 6,
         scratch_shapes=[
+            pltpu.VMEM((NY * 2, 16, width), BF16),
+            pltpu.VMEM((NY * 2, CAP, width), BF16),
+            pltpu.VMEM((NY * 2 * CAP, count), BF16),
+            pltpu.VMEM(hidden.shape, BF16),
+            pltpu.VMEM(grad.shape, BF16),
             pltpu.VMEM((2, slots, 16, width), BF16),
             pltpu.VMEM(wgu.shape, BF16),
             pltpu.VMEM(wd.shape, BF16),
@@ -632,11 +720,14 @@
             dma((2,)),
             dma((4,)),
             dma((4,)),
+            dma((2,)),
+            dma((1,)),
+            dma((1,)),
         ],
         compiler_params=pltpu.CompilerParams(
             collective_id=0, has_side_effects=True, vmem_limit_bytes=60 * 1024 * 1024
         ),
-    )(mine, wgu, wd, hidden, grad, gain, place)
+    )(ids, weights, gain_row, wgu, wd, hidden, grad, gain)
 
 
 def finish_kernel(
@@ -645,11 +736,15 @@
     grad_hbm,
     place_ref,
     gain_ref,
+    ids_ref,
+    weight_ref,
+    dc_ref,
     ggu_hbm,
     gd_hbm,
     handed_hbm,
     ggu_out,
     gd_out,
+    combine_ref,
     back,
     hidden,
     grad,
@@ -676,6 +771,14 @@
     ]
     for copy in ins:
         copy.start()
+    ids = ids_ref[...]
+    weights = weight_ref[...].astype(F32)
+    plain, _ = placing(ids, weights)
+    total = jnp.zeros(ids.shape, F32)
+    for e in range(NY * 2):
+        dc = jnp.sum(plain[e] * dc_ref[e].astype(F32), axis=0, keepdims=True)
+        total = total + jnp.where(ids == e, dc, 0.0)
+    combine_ref[...] = total / weights
     ins[0].wait()
     tile = 512
     square = jnp.zeros((count, 128), F32)
@@ -714,16 +817,16 @@
         copy.wait()
 
 
-def finish(back, hidden, grad, place, gain, ggu, gd):
+def finish(back, hidden, grad, place, gain, ids, weights, dc, ggu, gd):
     like = lambda array: jax.ShapeDtypeStruct(array.shape, array.dtype)
     hbm = pl.BlockSpec(memory_space=pl.ANY)
     vmem = pl.BlockSpec(memory_space=pltpu.VMEM)
     room = lambda array: pltpu.VMEM(array.shape, array.dtype)
     return pl.pallas_call(
         finish_kernel,
-        out_shape=(like(hidden), like(ggu), like(gd)),
-        in_specs=[hbm, hbm, hbm, vmem, vmem, hbm, hbm],
-        out_specs=[hbm, hbm, hbm],
+        out_shape=(like(hidden), like(ggu), like(gd), jax.ShapeDtypeStruct(ids.shape, F32)),
+        in_specs=[hbm, hbm, hbm, vmem, vmem, vmem, vmem, vmem, hbm, hbm],
+        out_specs=[hbm, hbm, hbm, vmem],
         scratch_shapes=[
             room(back),
             room(hidden),
@@ -736,67 +839,40 @@
             pltpu.SemaphoreType.DMA((3,)),
         ],
         compiler_params=pltpu.CompilerParams(vmem_limit_bytes=63 * 1024 * 1024),
-    )(back, hidden, grad, place, gain, ggu, gd)
+    )(back, hidden, grad, place, gain, ids, weights, dc, ggu, gd)
 
 
 def on_device(hidden_in, out_grad, expert_ids, route_weight, norm_gain, w_gate_up, w_down):
-    tokens_in = hidden_in[0]
-    grad_out = out_grad[0]
-    chosen = expert_ids[0]
-    weights_in = route_weight[0]
-    gain_row = norm_gain[0]
-    devices = lax.axis_size("expert")
-    span = devices // SPLIT
-    width = tokens_in.shape[1]
-    core = lax.rem(lax.axis_index("expert"), 2)
-    pairs = [(i, i ^ 1) for i in range(devices)]
-
-    tokens_f = tokens_in.astype(F32)
-    rms_value = jnp.sqrt(jnp.mean(tokens_f * tokens_f, axis=-1, keepdims=True) + 1e-06)
-    normed = tokens_f / rms_value
-    normed_in = (normed * gain_row).astype(BF16)
-    expert_range = jnp.arange(span, dtype=jnp.int32)
-    picked = chosen[:, :, None] == expert_range[None, None, :]
-    member = jnp.any(picked, axis=1).astype(jnp.int32)
-    weight_te = jnp.sum(jnp.where(picked, weights_in.astype(F32)[:, :, None], 0.0), axis=1)
-    position = jnp.cumsum(member, axis=0) - member
-    slot_range = jnp.arange(CAP, dtype=jnp.int32)
-    placing = (position.T[:, None, :] == slot_range[None, :, None]) & (member.T[:, None, :] == 1)
-    place_f = placing.astype(F32)
-    place_bf = placing.astype(BF16)
-    place_w = (place_f * weight_te.T[:, None, :]).astype(BF16)
-    sent_in = jnp.einsum("wst,td->wsd", place_bf, normed_in, preferred_element_type=F32).astype(BF16)
-    sent_grad = jnp.einsum("wst,td->wsd", place_w, grad_out, preferred_element_type=F32).astype(BF16)
-    keep = jnp.where(core == 0, sent_in, sent_grad)
-    give = jnp.where(core == 0, sent_grad, sent_in)
-    got = lax.ppermute(give, "expert", pairs)
-    first = jnp.where(core == 0, keep, got)
-    second = jnp.where(core == 0, got, keep)
-    mine = jnp.concatenate([first, second], axis=1)
-
+    width = hidden_in.shape[2]
+    ids = expert_ids[0].T
+    weights = route_weight[0].T
     back, dc_back, ggu, gd, hidden_next, grad_next, gain_next, place_next = experts(
-        mine,
+        ids,
+        weights,
+        norm_gain,
         w_gate_up[0, 0],
         w_down[0, 0],
-        tokens_in,
-        grad_out,
-        gain_row.reshape(-1, 128),
-        place_bf.reshape(span * CAP, -1),
+        hidden_in[0],
+        out_grad[0],
+        norm_gain.reshape(-1, 128),
     )
-
-    handed, grad_gate_up, grad_down = finish(
-        back, hidden_next, grad_next, place_next, gain_next.reshape(1, width), ggu, gd
+    handed, grad_gate_up, grad_down, combine = finish(
+        back,
+        hidden_next,
+        grad_next,
+        place_next,
+        gain_next.reshape(1, width),
+        ids,
+        weights,
+        dc_back,
+        ggu,
+        gd,
     )
-
-    comb_rows = dc_back[:, :, 0].astype(F32)
-    comb_te = jnp.sum(place_f * comb_rows[:, :, None], axis=1)
-    comb_te = comb_te / jnp.where(member.T == 1, weight_te.T, 1.0)
-    grad_combine = jnp.sum(jnp.where(picked, comb_te.T[:, None, :], 0.0), axis=-1)
     return (
         handed[None],
         grad_gate_up[None, None],
         grad_down[None, None],
-        grad_combine[None],
+        combine.T[None],
     )
 
 

time: 140 us -> 132 us (0.943); the launches traced: 140 us -> 130 us
  other arithmetic: 7.19 us -> 0 us
  matrix products: 2.12 us -> 0 us
    reduce_sum x4 -> x0, other arithmetic: 2.96 us -> none  [the longest x1 1.54 us: on_device(): jnp.mean(tokens_f * tokens_f, axis=-1, keepdims=True) + 1e-06]
    dot_general x2 -> x0, matrix products: 2.12 us -> none  [the longest x1 1.83 us: on_device(): jnp.einsum('wst,td->wsd', place_bf, normed_in, preferred_element_type=F32)]
  transfers between devices with their start and end apart: 1 -> 0, of which waited for: 1 -> 0; matrix products, arithmetic and copies ran while one was open for 1% -> 0% of each run, Pallas kernels for 0% -> 0%
where the time goes in v7:
time: 132 us; the launch traced here: 130 us
  Pallas kernels  129 us (98%)
    pallas_call x1, Pallas kernels, experts(): pl.pallas_call(expert_kernel, out_shape=(jax.ShapeDtypeStruct((NY * 2, CA...  122 us
    pallas_call x1, Pallas kernels, finish(): pl.pallas_call(finish_kernel, out_shape=(like(hidden), like(ggu), like(gd...  7.11 us

profile of v7, /device:TPU:25, one launch (start us, length us, event | category | flops | bytes accessed | tf_op | source)
XLA Modules:
  0.0 129.8 jit_solution(5384814186848827607)
XLA Ops:
  0.6 122.1 %shard_map.102 = (bf16[8,8,4352]{2,1,0:T(8,128)(2,1)}, bf16[8,8,128]{2,1,0:T(8,128)(2,1)}, bf16[2,192,4096]{2,1,0:T(8,128)(2,1)}, bf16[192,4096]{1,0:T(8,128)(2,...) custom-call(s32[8,128]{1,0:T(8,128)} %bitcast.24, ...), custom_call_target="tpu_custom_call" | custom-call | tf_op jit(solution)/shard_map/pallas_call | solution.py:671
  122.7 7.1 %shard_map.103 = (bf16[128,4096]{1,0:T(8,128)(2,1)}, bf16[2,192,4096]{2,1,0:T(8,128)(2,1)}, bf16[192,4096]{1,0:T(8,128)(2,1)}, f32[8,128]{1,0:T(8,128)}) custom-call(bf16[8,8,4352]{2,1,0:T(8,128)(2,1)} %get-tuple-element.16.back_hbm, bf16[128,4096]{1,0:T(8,128)(2,1)} %get-tuple-element.17.hidden_hbm, bf16[128,4096]{1,0:T(8,128)(2,1)} %get-tuple-element.18.grad_hbm, ...), custom_call_target="tpu_custom_call" | custom-call | tf_op jit(solution)/shard_map/pallas_call | solution.py:825

commit v8 on v7

--- a/solution.py
+++ b/solution.py
@@ -195,10 +195,10 @@
     for n in range(width // 128):
         h = tokens[:, n * 128 : (n + 1) * 128].astype(F32)
         square = square + h * h
-    rms = jnp.sqrt(jnp.sum(square, axis=1, keepdims=True) / width + 1e-06)
+    scale = 1.0 / jnp.sqrt(jnp.sum(square, axis=1, keepdims=True) / width + 1e-06)
     for n in range(width // 512):
         cols = slice(n * 512, (n + 1) * 512)
-        u = ((tokens[:, cols].astype(F32) / rms) * gain_row[:, cols]).astype(BF16)
+        u = ((tokens[:, cols].astype(F32) * scale) * gain_row[:, cols]).astype(BF16)
         sent_in = nn(place, u).astype(BF16).reshape(NY * 2, CAP, 512)
         sent_grad = nn(place_w, token_grad[:, cols]).astype(BF16).reshape(NY * 2, CAP, 512)
 
@@ -226,20 +226,26 @@
             device_id_type=MESH,
         )
 
-    def give_copy(place_of):
+    def give_copy(e, place_of):
         return remote(
-            give, mine_ref.at[:, pl.ds(place_of * CAP, CAP)], give_send.at[0], give_recv.at[0], partner
-        )
-
-    @pl.when(core == 0)
-    def _():
-        give_copy(0).start()
-
-    @pl.when(core == 1)
-    def _():
-        give_copy(1).start()
-
-    give_copy(0).wait()
+            give.at[e],
+            mine_ref.at[e, pl.ds(place_of * CAP, CAP)],
+            give_send.at[e],
+            give_recv.at[e],
+            partner,
+        )
+
+    for step in range(NY):
+        yy = lax.rem(y + step, NY)
+        for e in (yy * 2 + half, yy * 2 + 1 - half):
+
+            @pl.when(core == 0)
+            def _():
+                give_copy(e, 0).start()
+
+            @pl.when(core == 1)
+            def _():
+                give_copy(e, 1).start()
 
     slot = z * NY + y
 
@@ -249,19 +255,22 @@
         )
 
     own_copy = pltpu.make_async_copy(mine_ref.at[expert], rows.at[core, slot], row_sem.at[slot])
-    own_copy.start()
-    for step in range(NY):
-        yy = lax.rem(y + step, NY)
-        if step > 0:
-            entry(yy * 2 + half, step, at(yy, z, core)).start()
 
     def entry_far(step):
         yy = lax.rem(y + step, NY)
         return entry(yy * 2 + 1 - half, NY + step, at(yy, entry_z, core))
 
-    @pl.when(jnp.logical_not(at_end))
-    def _():
-        for step in range(NY):
+    for step in range(NY):
+        yy = lax.rem(y + step, NY)
+        give_copy(yy * 2 + half, 0).wait()
+        if step > 0:
+            entry(yy * 2 + half, step, at(yy, z, core)).start()
+        else:
+            own_copy.start()
+        give_copy(yy * 2 + 1 - half, 0).wait()
+
+        @pl.when(jnp.logical_not(at_end))
+        def _():
             entry_far(step).start()
 
     early = [
@@ -572,7 +581,7 @@
 
         @pl.loop(0, 4)
         def _(s):
-            n = 4 * (it - 13) + s
+            n = jnp.where(at_end, 4 * (it - 13) + s, jnp.where(s < 2, 2 * (it - 9) + s, -1))
             tile = 512
 
             @pl.when((n >= 0) & (n < width // tile))
@@ -721,8 +730,8 @@
             dma((4,)),
             dma((4,)),
             dma((2,)),
-            dma((1,)),
-            dma((1,)),
+            dma((2 * NY,)),
+            dma((2 * NY,)),
         ],
         compiler_params=pltpu.CompilerParams(
             collective_id=0, has_side_effects=True, vmem_limit_bytes=60 * 1024 * 1024
@@ -785,7 +794,15 @@
     for n in range(width // 128):
         h = hidden[:, n * 128 : (n + 1) * 128].astype(F32)
         square = square + h * h
-    rms = jnp.sqrt(jnp.sum(square, axis=1, keepdims=True) / width + 1e-06)
+    scale = 1.0 / jnp.sqrt(jnp.sum(square, axis=1, keepdims=True) / width + 1e-06)
+    for i in (3, 4):
+        ins[i].wait()
+    grads = [
+        pltpu.make_async_copy(ggu, ggu_out, out_sem.at[0]),
+        pltpu.make_async_copy(gd, gd_out, out_sem.at[1]),
+    ]
+    for copy in grads:
+        copy.start()
     ins[1].wait()
     place = place_ref[...]
     along = jnp.zeros((count, 1), F32)
@@ -794,26 +811,25 @@
         rows = back[:, :, 128 + n * tile : 128 + (n + 1) * tile].reshape(-1, tile)
         part = tn(place, rows) * gain_ref[:, cols]
         scaled[:, cols] = part
-        along = along + jnp.sum(part * (hidden[:, cols].astype(F32) / rms), axis=1, keepdims=True)
-    inner = along / width
-    for i in (3, 4):
-        ins[i].wait()
-    outs = [
-        pltpu.make_async_copy(ggu, ggu_out, out_sem.at[0]),
-        pltpu.make_async_copy(gd, gd_out, out_sem.at[1]),
-        pltpu.make_async_copy(handed, handed_hbm, out_sem.at[2]),
-    ]
-    outs[0].start()
-    outs[1].start()
+        along = along + jnp.sum(part * hidden[:, cols].astype(F32), axis=1, keepdims=True)
+    inner = along * scale / width
     ins[2].wait()
+    halves = []
     for n in range(width // tile):
         cols = slice(n * tile, (n + 1) * tile)
-        normed = hidden[:, cols].astype(F32) / rms
+        normed = hidden[:, cols].astype(F32) * scale
         handed[:, cols] = (
-            grad[:, cols].astype(F32) + (scaled[:, cols] - normed * inner) / rms
+            grad[:, cols].astype(F32) + (scaled[:, cols] - normed * inner) * scale
         ).astype(BF16)
-    outs[2].start()
-    for copy in outs:
+        if n in (width // tile // 2 - 1, width // tile - 1):
+            span = pl.ds(len(halves) * (width // 2), width // 2)
+            halves.append(
+                pltpu.make_async_copy(
+                    handed.at[:, span], handed_hbm.at[:, span], out_sem.at[2 + len(halves)]
+                )
+            )
+            halves[-1].start()
+    for copy in grads + halves:
         copy.wait()
 
 
@@ -836,7 +852,7 @@
             room(gd),
             pltpu.VMEM(hidden.shape, F32),
             pltpu.SemaphoreType.DMA((5,)),
-            pltpu.SemaphoreType.DMA((3,)),
+            pltpu.SemaphoreType.DMA((4,)),
         ],
         compiler_params=pltpu.CompilerParams(vmem_limit_bytes=63 * 1024 * 1024),
     )(back, hidden, grad, place, gain, ids, weights, dc, ggu, gd)

time: 132 us -> 130 us (0.985); the launches traced: 130 us -> 129 us
  no operation moved by 1% of the time
where the time goes in v8:
time: 130 us; the launch traced here: 129 us
  Pallas kernels  129 us (99%)
    pallas_call x1, Pallas kernels, experts(): pl.pallas_call(expert_kernel, out_shape=(jax.ShapeDtypeStruct((NY * 2, CA...  122 us
    pallas_call x1, Pallas kernels, finish(): pl.pallas_call(finish_kernel, out_shape=(like(hidden), like(ggu), like(gd...  7.1 us

profile of v8, /device:TPU:25, one launch (start us, length us, event | category | flops | bytes accessed | tf_op | source)
XLA Modules:
  0.0 129.3 jit_solution(15830983397858936208)
XLA Ops:
  0.6 121.6 %shard_map.102 = (bf16[8,8,4352]{2,1,0:T(8,128)(2,1)}, bf16[8,8,128]{2,1,0:T(8,128)(2,1)}, bf16[2,192,4096]{2,1,0:T(8,128)(2,1)}, bf16[192,4096]{1,0:T(8,128)(2,...) custom-call(s32[8,128]{1,0:T(8,128)} %bitcast.24, ...), custom_call_target="tpu_custom_call" | custom-call | tf_op jit(solution)/shard_map/pallas_call | solution.py:680
  122.2 7.1 %shard_map.103 = (bf16[128,4096]{1,0:T(8,128)(2,1)}, bf16[2,192,4096]{2,1,0:T(8,128)(2,1)}, bf16[192,4096]{1,0:T(8,128)(2,1)}, f32[8,128]{1,0:T(8,128)}) custom-call(bf16[8,8,4352]{2,1,0:T(8,128)(2,1)} %get-tuple-element.16.back_hbm, bf16[128,4096]{1,0:T(8,128)(2,1)} %get-tuple-element.17.hidden_hbm, bf16[128,4096]{1,0:T(8,128)(2,1)} %get-tuple-element.18.grad_hbm, ...), custom_call_target="tpu_custom_call" | custom-call | tf_op jit(solution)/shard_map/pallas_call | solution.py:841

commit v9 on v8

--- a/solution.py
+++ b/solution.py
@@ -579,9 +579,10 @@
         def _():
             combine(z, 0, 0)
 
-        @pl.loop(0, 4)
+        @pl.loop(0, 6)
         def _(s):
-            n = jnp.where(at_end, 4 * (it - 13) + s, jnp.where(s < 2, 2 * (it - 9) + s, -1))
+            few = jnp.where(s < 2, jnp.where(at_end, s - 100 * (13 - it), 2 * (it - 9) + s), -1)
+            n = jnp.where(at_end & (it == 14), 2 + s, few)
             tile = 512
 
             @pl.when((n >= 0) & (n < width // tile))

time: 130 us -> 131 us (level)
  no operation moved by 1% of the time
where the time goes in v9:
time: 131 us; the launch traced here: 129 us
  Pallas kernels  129 us (98%)
    pallas_call x1, Pallas kernels, experts(): pl.pallas_call(expert_kernel, out_shape=(jax.ShapeDtypeStruct((NY * 2, CA...  122 us
    pallas_call x1, Pallas kernels, finish(): pl.pallas_call(finish_kernel, out_shape=(like(hidden), like(ggu), like(gd...  7.1 us

profile of v9, /device:TPU:25, one launch (start us, length us, event | category | flops | bytes accessed | tf_op | source)
XLA Modules:
  0.0 129.3 jit_solution(4127723220691210341)
XLA Ops:
  0.6 121.6 %shard_map.102 = (bf16[8,8,4352]{2,1,0:T(8,128)(2,1)}, bf16[8,8,128]{2,1,0:T(8,128)(2,1)}, bf16[2,192,4096]{2,1,0:T(8,128)(2,1)}, bf16[192,4096]{1,0:T(8,128)(2,...) custom-call(s32[8,128]{1,0:T(8,128)} %bitcast.24, ...), custom_call_target="tpu_custom_call" | custom-call | tf_op jit(solution)/shard_map/pallas_call | solution.py:681
  122.2 7.1 %shard_map.103 = (bf16[128,4096]{1,0:T(8,128)(2,1)}, bf16[2,192,4096]{2,1,0:T(8,128)(2,1)}, bf16[192,4096]{1,0:T(8,128)(2,1)}, f32[8,128]{1,0:T(8,128)}) custom-call(bf16[8,8,4352]{2,1,0:T(8,128)(2,1)} %get-tuple-element.16.back_hbm, bf16[128,4096]{1,0:T(8,128)(2,1)} %get-tuple-element.17.hidden_hbm, bf16[128,4096]{1,0:T(8,128)(2,1)} %get-tuple-element.18.grad_hbm, ...), custom_call_target="tpu_custom_call" | custom-call | tf_op jit(solution)/shard_map/pallas_call | solution.py:842
